TPU v7x, 32 devices: a whole 2x2x4 slice. The times are simulated.
32 devices in a mesh: gx: 4 (over y, x), gy: 4 (over z), gz: 2 (over core).
Axes of the slice: x: 2, y: 2, z: 4, core: 2. Of those that a mesh axis runs over, the one named last changes fastest.
Arguments:
- fields: float32 [24, 32, 128, 256], P(None, 'gx', 'gy', 'gz'), may hold values from -8.5 to 8.5
- velocity: float32 [3, 32, 128, 256], P(None, 'gx', 'gy', 'gz'), may hold values from -0.4 to 0.4
- diffusivity: float32 [24], replicated, may hold values from 0.02 to 0.15
- weight_in: bfloat16 [24, 1600], replicated, may hold values from -1.25 to 1.25
- bias_in: float32 [1600], replicated, may hold values from -3 to 3
- weight_mid: bfloat16 [1600, 800], replicated, may hold values from -0.15625 to 0.15625
- bias_mid: float32 [800], replicated, may hold values from -3 to 3
- weight_low: bfloat16 [800, 400], replicated, may hold values from -0.21875 to 0.21875
- bias_low: float32 [400], replicated, may hold values from -3 to 3
- weight_out: bfloat16 [400, 24], replicated, may hold values from -0.3125 to 0.3125
- bias_out: float32 [24], replicated, may hold values from -3 to 3
- react_list: int32 [32, 96], P(('gx', 'gy', 'gz')), may hold values from -1 to 255, as said below
- owner_table: int32 [32, 96], P(('gx', 'gy', 'gz')), may hold values from -1 to 31, as said below
Outputs:
- updated: float32 [24, 32, 128, 256], P(None, 'gx', 'gy', 'gz')
- owner_activity: float32 [32], P(('gx', 'gy', 'gz'))
Inputs may be any that keep to these rules, and one draw needn't show every extreme that they name: `react_list`: row d lists distinct blocks of brick d, valid entries first and -1 after them; a brick lists at most 96 blocks and some brick lists exactly 96; all bricks together list 32 times the number of devices. owner_table[d, i] is -1 exactly where react_list[d, i] is, else the owner's index over gx+gy+gz; every device owns exactly 32 blocks; no brick sends more than 3 blocks to one owner, and some brick sends exactly 3 to some owner.
All inputs are finite; a program needn't handle non-finite values.
Results may differ from a plain program's by a relative error of at most 0.00058.
Values may be sent and summed in bfloat16 or wider, within the bound.
A program may use at most 256 MiB of HBM per device.

v0:
```python
import functools

import jax
import jax.numpy as jnp
from jax import lax
from jax.experimental import pallas as pl
from jax.experimental.pallas import tpu as pltpu
from jax.sharding import PartitionSpec as P

AXES = ("gx", "gy", "gz")
MESH = pl.DeviceIdType.MESH
SUB = 8
LANES = 128
VMEM_LIMIT = 60 * 1024 * 1024


def neighbours():
    ids = {a: lax.axis_index(a) for a in AXES}
    out = []
    for a in AXES:
        n = lax.axis_size(a)
        up = dict(ids)
        up[a] = lax.rem(ids[a] + 1, n)
        down = dict(ids)
        down[a] = lax.rem(ids[a] + n - 1, n)
        out.append((tuple(up[b] for b in AXES), tuple(down[b] for b in AXES)))
    return out


def enter(targets):
    barrier = pltpu.get_barrier_semaphore()
    for to in targets:
        pl.semaphore_signal(barrier, inc=1, device_id=to, device_id_type=MESH)
    pl.semaphore_wait(barrier, len(targets))


def peers(axis):
    ids = {a: lax.axis_index(a) for a in AXES}
    n = lax.axis_size(axis)
    out = []
    for k in range(1, n):
        to = dict(ids)
        to[axis] = lax.rem(ids[axis] + k, n)
        out.append(tuple(to[b] for b in AXES))
    return out


class Halo:
    def __init__(self, near, cx, cy, xs, xr, yr, zs, zr, send_sem, recv_sem):
        self.near, self.cx, self.cy = near, cx, cy
        self.xs, self.xr, self.yr, self.zs, self.zr = xs, xr, yr, zs, zr
        self.send_sem, self.recv_sem = send_sem, recv_sem

    def copies(self, slot, u):
        cx, cy = self.cx, self.cy
        (xu, xd), (yu, yd), (zu, zd) = self.near
        plan = [
            (self.xs.at[slot, 1], self.xr.at[slot, 0], xu),
            (self.xs.at[slot, 0], self.xr.at[slot, 1], xd),
            (u.at[pl.ds(1, cx), cy], self.yr.at[slot, 0], yu),
            (u.at[pl.ds(1, cx), 1], self.yr.at[slot, 1], yd),
            (self.zs.at[slot, 1], self.zr.at[slot, 0], zu),
            (self.zs.at[slot, 0], self.zr.at[slot, 1], zd),
        ]
        return [
            pltpu.make_async_remote_copy(
                src_ref=s, dst_ref=d, send_sem=self.send_sem.at[slot, i],
                recv_sem=self.recv_sem.at[slot, i], device_id=to, device_id_type=MESH)
            for i, (s, d, to) in enumerate(plan)
        ]

    def send(self, slot, u):
        for side, x in ((0, 1), (1, self.cx)):
            for k in range(self.cy // 2):
                pair = jnp.concatenate([u[x, 1 + 2 * k], u[x, 2 + 2 * k]], axis=0)
                self.xs[slot, side, k] = pair.astype(jnp.bfloat16)
        for c in self.copies(slot, u):
            c.start()

    def receive(self, slot, u):
        for c in self.copies(slot, u):
            c.wait_recv()
        for side, x in ((0, 0), (1, self.cx + 1)):
            for k in range(self.cy // 2):
                pair = self.xr[slot, side, k].astype(jnp.float32)
                u[x, 1 + 2 * k] = pair[:SUB]
                u[x, 2 + 2 * k] = pair[SUB:]
        for side, y in ((0, 0), (1, self.cy + 1)):
            for x in range(self.cx):
                u[1 + x, y] = self.yr[slot, side, x]

    def finish(self, slot, u):
        for c in self.copies(slot, u):
            c.wait_send()


def lane_ids():
    return lax.broadcasted_iota(jnp.int32, (SUB, LANES), 1)


def face_add(lane, y, t, low, high):
    low = jnp.where(lane == y, pltpu.roll(t, y, 1) if y else t, low)
    high = jnp.where(lane == y, pltpu.roll(t, y + 1, 1), high)
    return low, high


def z_near(lane, y, t, zr_low, zr_high):
    last = pltpu.roll(zr_high, LANES - 1 - y, 1)
    first = pltpu.roll(zr_low, LANES - y, 1) if y else zr_low
    after = jnp.where(lane == LANES - 1, last, pltpu.roll(t, LANES - 1, 1))
    before = jnp.where(lane == 0, first, pltpu.roll(t, 1, 1))
    return after, before


def load_chunk(halo, slot, src, u):
    lane = lane_ids()

    def body(x, _):
        low = jnp.zeros((SUB, LANES), jnp.float32)
        high = low
        for y in range(halo.cy):
            t = src[x, y]
            u[1 + x, 1 + y] = t
            low, high = face_add(lane, y, t, low, high)
        halo.zs[slot, 0, x] = low
        halo.zs[slot, 1, x] = high
        return 0

    lax.fori_loop(0, halo.cx, body, 0)


def flow_kernel(chunks, cx, cy, q_ref, v_ref, out_ref, u_ref, w_ref, coef,
                xs, xr, yr, zs, zr, send_sem, recv_sem):
    near = neighbours()
    enter([to for pair in near for to in pair])
    halo = Halo(near, cx, cy, xs, xr, yr, zs, zr, send_sem, recv_sem)
    lane = lane_ids()
    v_slot = 3 * chunks
    load_chunk(halo, v_slot, v_ref, w_ref)
    halo.send(v_slot, w_ref)
    for c in range(chunks):
        load_chunk(halo, c, q_ref.at[c], u_ref.at[0, c])
        halo.send(c, u_ref.at[0, c])
    halo.receive(v_slot, w_ref)

    def make_coef(x, _):
        zl, zh = zr[v_slot, 0, x], zr[v_slot, 1, x]
        for y in range(cy):
            t = w_ref[1 + x, 1 + y]
            za, zb = z_near(lane, y, t, zl, zh)
            rows = (
                0.05 - 0.5 * w_ref[2 + x, 1 + y][0:1],
                0.05 + 0.5 * w_ref[x, 1 + y][0:1],
                0.05 - 0.5 * w_ref[1 + x, 2 + y][1:2],
                0.05 + 0.5 * w_ref[1 + x, y][1:2],
                0.05 - 0.5 * za[2:3],
                0.05 + 0.5 * zb[2:3],
            )
            for i, r in enumerate(rows):
                coef[i, x, y] = jnp.broadcast_to(r, (SUB, LANES))
        return 0

    lax.fori_loop(0, cx, make_coef, 0)

    for stage in range(3):
        weight = (1.0 / 3.0, 0.5, 1.0)[stage]
        for c in range(chunks):
            slot = stage * chunks + c
            u = u_ref.at[stage, c]
            halo.receive(slot, u)

            def body(x, _):
                zl, zh = zr[slot, 0, x], zr[slot, 1, x]
                low = jnp.zeros((SUB, LANES), jnp.float32)
                high = low
                for y in range(cy):
                    t = u[1 + x, 1 + y]
                    za, zb = z_near(lane, y, t, zl, zh)
                    s = coef[0, x, y] * u[2 + x, 1 + y] + coef[1, x, y] * u[x, 1 + y]
                    s = s + (coef[2, x, y] * u[1 + x, 2 + y] + coef[3, x, y] * u[1 + x, y])
                    s = s + (coef[4, x, y] * za + coef[5, x, y] * zb)
                    r = q_ref[c, x, y] + weight * (s - 0.3 * t)
                    if stage == 2:
                        out_ref[c, x, y] = r
                    else:
                        u_ref[stage + 1, c, 1 + x, 1 + y] = r
                        low, high = face_add(lane, y, r, low, high)
                if stage < 2:
                    zs[slot + chunks, 0, x] = low
                    zs[slot + chunks, 1, x] = high
                return 0

            lax.fori_loop(0, cx, body, 0)
            if stage < 2:
                halo.send(slot + chunks, u_ref.at[stage + 1, c])
    for stage in range(3):
        for c in range(chunks):
            halo.finish(stage * chunks + c, u_ref.at[stage, c])
    halo.finish(v_slot, w_ref)


def diffuse_kernel(chunks, cx, cy, q_ref, d_ref, act_in, out_ref, act_out, u_ref, part, got,
                   act_send, act_recv, xs, xr, yr, zs, zr, send_sem, recv_sem):
    near = neighbours()
    groups = [peers(a) for a in AXES[::-1]]
    enter([to for g in groups for to in g])
    halo = Halo(near, cx, cy, xs, xr, yr, zs, zr, send_sem, recv_sem)
    lane = lane_ids()

    def hops(phase):
        return [
            pltpu.make_async_remote_copy(
                src_ref=part.at[phase], dst_ref=got.at[phase, k],
                send_sem=act_send.at[phase, k], recv_sem=act_recv.at[phase, k],
                device_id=to, device_id_type=MESH)
            for k, to in enumerate(groups[phase])
        ]

    def gather(phase):
        for h in hops(phase):
            h.wait_recv()
        total = part[phase]
        for k in range(len(groups[phase])):
            total = total + got[phase, k]
        return total

    part[0] = act_in[...]
    for c in range(chunks):
        load_chunk(halo, c, q_ref.at[c], u_ref.at[c])
        halo.send(c, u_ref.at[c])
        if c == 0:
            for h in hops(0):
                h.start()
    for c in range(chunks):
        u = u_ref.at[c]
        if c < len(groups) - 1:
            part[c + 1] = gather(c)
            for h in hops(c + 1):
                h.start()
        halo.receive(c, u)
        rate = d_ref[c]

        def body(x, _):
            zl, zh = zr[c, 0, x], zr[c, 1, x]
            for y in range(cy):
                t = u[1 + x, 1 + y]
                za, zb = z_near(lane, y, t, zl, zh)
                s = (u[2 + x, 1 + y] + u[x, 1 + y]) + (u[1 + x, 2 + y] + u[1 + x, y])
                s = s + (za + zb)
                out_ref[c, x, y] = t + rate * (s - 6.0 * t)
            return 0

        lax.fori_loop(0, cx, body, 0)
    done = min(chunks, len(groups) - 1)
    for phase in range(done, len(groups) - 1):
        part[phase + 1] = gather(phase)
        for h in hops(phase + 1):
            h.start()
    total = gather(len(groups) - 1)
    me = (lax.axis_index("gx") * lax.axis_size("gy") + lax.axis_index("gy")) * lax.axis_size(
        "gz") + lax.axis_index("gz")
    flat = lax.broadcasted_iota(jnp.int32, (SUB, LANES), 0) * LANES + lane
    mine = jnp.where(flat == me, total, 0.0)
    act_out[...] = jnp.broadcast_to(
        jnp.sum(jnp.sum(mine, axis=1, keepdims=True), axis=0, keepdims=True), (SUB, LANES))
    for phase in range(len(groups)):
        for h in hops(phase):
            h.wait_send()
    for c in range(chunks):
        halo.finish(c, u_ref.at[c])


def chem_kernel(chunks, cy, group, list_ref, owner_ref, q_ref, w1, w2, w3, w4,
                out_ref, act_ref, x_in, h1, h2, h3, inc):
    listed = list_ref.shape[0]
    n_lanes = group * LANES
    out_ref[...] = q_ref[...]
    act_ref[...] = jnp.zeros_like(act_ref)
    flat = (lax.broadcasted_iota(jnp.int32, (SUB, LANES), 0) * LANES + lane_ids())
    row = lax.broadcasted_iota(jnp.int32, (16, n_lanes), 0)
    ones = jnp.where(row < 3, 1.0, 0.0)
    fields = chunks * SUB
    x_in[fields:fields + SUB] = ones[:SUB]
    for h in (h1, h2, h3):
        h[h.shape[0] - 16:] = ones.astype(jnp.bfloat16)
    count = lax.fori_loop(
        0, listed, lambda i, n: n + jnp.where(list_ref[i] >= 0, 1, 0), 0)

    def layer(w, src, dst, step):
        rows = w.shape[0]
        for m in range(0, rows, step):
            k = min(step, rows - m)
            h = jnp.dot(w[m:m + k], src, preferred_element_type=jnp.float32)
            dst[m:m + k] = (h + h * jnp.tanh(h)).astype(jnp.bfloat16)

    def run(g, _):
        base = g * group
        for i in range(group):
            b = jnp.maximum(list_ref[base + i], 0)
            x, y = b // cy, lax.rem(b, cy)
            for c in range(chunks):
                x_in[c * SUB:(c + 1) * SUB, i * LANES:(i + 1) * LANES] = q_ref[c, x, y]
        layer(w1, x_in[...].astype(jnp.bfloat16), h1, 400)
        layer(w2, h1[...], h2, 400)
        layer(w3, h2[...], h3, 400)
        inc[...] = jnp.dot(w4[...], h3[...], preferred_element_type=jnp.float32)
        for i in range(group):
            entry = list_ref[base + i]
            b = jnp.maximum(entry, 0)
            valid = jnp.where(entry >= 0, 1.0, 0.0)
            x, y = b // cy, lax.rem(b, cy)
            for c in range(chunks):
                t = inc[c * SUB:(c + 1) * SUB, i * LANES:(i + 1) * LANES]
                out_ref[c, x, y] = out_ref[c, x, y] + valid * t
            r = inc[0:1, i * LANES:(i + 1) * LANES]
            heat = jnp.sum(r * r, axis=1, keepdims=True) * (valid / (8.0 * LANES))
            act_ref[...] = act_ref[...] + jnp.where(flat == owner_ref[base + i], heat, 0.0)
        return 0

    lax.fori_loop(0, (count + group - 1) // group, run, 0)


def bias_columns(bias, scale):
    rest = bias * scale
    columns = []
    for _ in range(3):
        part = lax.reduce_precision(rest, 8, 7)
        rest = rest - part
        columns.append(part)
    columns = jnp.stack(columns, axis=1).astype(jnp.bfloat16)
    return columns


def folded(weight, bias, scale, pad):
    cols = bias_columns(bias, scale)
    cols = jnp.pad(cols, ((0, 0), (0, pad - 3)))
    return jnp.concatenate([weight.T * jnp.bfloat16(scale), cols], axis=1)


def vmem(n):
    return [pl.BlockSpec(memory_space=pltpu.VMEM)] * n


def halo_scratch(slots, cx, cy):
    return [
        pltpu.VMEM((slots, 2, cy // 2, 2 * SUB, LANES), jnp.bfloat16),
        pltpu.VMEM((slots, 2, cy // 2, 2 * SUB, LANES), jnp.bfloat16),
        pltpu.VMEM((slots, 2, cx, SUB, LANES), jnp.float32),
        pltpu.VMEM((slots, 2, cx, SUB, LANES), jnp.float32),
        pltpu.VMEM((slots, 2, cx, SUB, LANES), jnp.float32),
        pltpu.SemaphoreType.DMA((slots, 6)),
        pltpu.SemaphoreType.DMA((slots, 6)),
    ]


def local(fields, velocity, diffusivity, weight_in, bias_in, weight_mid, bias_mid,
          weight_low, bias_low, weight_out, bias_out, react_list, owner_table):
    nf, cx, cy, cz = fields.shape
    chunks = nf // SUB
    shape = (chunks, cx, cy, SUB, cz)
    q = fields.reshape(chunks, SUB, cx, cy, cz).transpose(0, 2, 3, 1, 4)
    v = jnp.pad(velocity, ((0, SUB - 3), (0, 0), (0, 0), (0, 0))).transpose(1, 2, 0, 3)
    padded = (cx + 2, cy + 2, SUB, cz)
    slots = 3 * chunks + 1
    flowed = pl.pallas_call(
        functools.partial(flow_kernel, chunks, cx, cy),
        out_shape=jax.ShapeDtypeStruct(shape, jnp.float32),
        in_specs=vmem(2),
        out_specs=vmem(1)[0],
        scratch_shapes=[
            pltpu.VMEM((3, chunks) + padded, jnp.float32),
            pltpu.VMEM(padded, jnp.float32),
            pltpu.VMEM((6, cx, cy, SUB, cz), jnp.float32),
        ] + halo_scratch(slots, cx, cy),
        compiler_params=pltpu.CompilerParams(
            collective_id=0, has_side_effects=True, vmem_limit_bytes=VMEM_LIMIT),
        name="flow",
    )(q, v)

    listed = react_list.shape[1]
    group = 4
    h = (weight_in.shape[1], weight_mid.shape[1], weight_low.shape[1])
    w1 = folded(weight_in, bias_in, 0.5, SUB)
    w2 = folded(weight_mid, bias_mid, 0.5, 16)
    w3 = folded(weight_low, bias_low, 0.5, 16)
    w4 = folded(weight_out, bias_out, 1.0, 16)
    smem = pl.BlockSpec(memory_space=pltpu.SMEM)
    n_lanes = group * LANES
    reacted, activity = pl.pallas_call(
        functools.partial(chem_kernel, chunks, cy, group),
        out_shape=(jax.ShapeDtypeStruct(shape, jnp.float32),
                   jax.ShapeDtypeStruct((SUB, LANES), jnp.float32)),
        in_specs=[smem, smem] + vmem(5),
        out_specs=tuple(vmem(2)),
        scratch_shapes=[
            pltpu.VMEM((nf + SUB, n_lanes), jnp.float32),
            pltpu.VMEM((h[0] + 16, n_lanes), jnp.bfloat16),
            pltpu.VMEM((h[1] + 16, n_lanes), jnp.bfloat16),
            pltpu.VMEM((h[2] + 16, n_lanes), jnp.bfloat16),
            pltpu.VMEM((nf, n_lanes), jnp.float32),
        ],
        compiler_params=pltpu.CompilerParams(vmem_limit_bytes=VMEM_LIMIT),
        name="chem",
    )(react_list[0], owner_table[0], flowed, w1, w2, w3, w4)

    rates = jnp.broadcast_to(diffusivity.reshape(chunks, SUB, 1), (chunks, SUB, cz))
    most = max(lax.axis_size(a) for a in AXES) - 1
    updated, mine = pl.pallas_call(
        functools.partial(diffuse_kernel, chunks, cx, cy),
        out_shape=(jax.ShapeDtypeStruct(shape, jnp.float32),
                   jax.ShapeDtypeStruct((SUB, LANES), jnp.float32)),
        in_specs=vmem(3),
        out_specs=tuple(vmem(2)),
        scratch_shapes=[
            pltpu.VMEM((chunks,) + padded, jnp.float32),
            pltpu.VMEM((len(AXES), SUB, LANES), jnp.float32),
            pltpu.VMEM((len(AXES), most, SUB, LANES), jnp.float32),
            pltpu.SemaphoreType.DMA((len(AXES), most)),
            pltpu.SemaphoreType.DMA((len(AXES), most)),
        ]
        + halo_scratch(chunks, cx, cy),
        compiler_params=pltpu.CompilerParams(
            collective_id=1, has_side_effects=True, vmem_limit_bytes=VMEM_LIMIT),
        name="diffuse",
    )(reacted, rates, activity)
    updated = updated.transpose(0, 3, 1, 2, 4).reshape(nf, cx, cy, cz)
    return (updated, mine[0, 0:1])


def solution(mesh):
    return jax.shard_map(
        local,
        mesh=mesh,
        in_specs=(P(None, *AXES), P(None, *AXES)) + (P(),) * 9
        + (P(AXES, None), P(AXES, None)),
        out_specs=(P(None, *AXES), P(AXES)),
        check_vma=False,
    )
```

profile of v0, /device:TPU:0, one launch (start us, length us, event | category | flops | bytes accessed | tf_op | source)
XLA Modules:
  0.0 172.6 jit_solution(14913159393306051633)
XLA Ops:
  0.6 6.3 %copy.44 = f32[3,8,8,32,128]{4,1,3,2,0:T(8,128)} copy(f32[3,8,8,32,128]{4,3,2,1,0:T(8,128)} %bitcast.25) | data formatting | bytes 6291456 | tf_op jit(solution)/shard_map/reshape | solution.py:361
  7.0 0.0 copy-done.2
  7.0 0.3 copy.37
  7.2 1.1 pad_bitcast_fusion.v_ref
  8.3 64.9 %flow.1.q_ref = f32[3,8,32,8,128]{4,3,2,1,0:T(8,128)} custom-call(f32[3,8,32,8,128]{4,3,2,1,0:T(8,128)} %bitcast.24, f32[8,32,8,128]{3,2,1,0:T(8,128)} %pad_bitcast_fusion.v_ref), custom_call_target="tpu_custom_call" | custom-call | tf_op jit(solution)/shard_map/flow/pallas_call | solution.py:365
  73.3 0.0 copy-done.3
  73.4 1.0 copy.41.w1
  74.4 0.0 copy-done.6
  74.4 0.2 copy.38
  74.6 0.3 multiply_bitcast_fusion
  74.9 0.0 copy-start.7
  74.9 0.0 copy-start.1
  74.9 1.8 %fusion.1.w2 = bf16[800,1616]{1,0:T(8,128)(2,1)} fusion(bf16[800,3]{1,0:T(8,128)(2,1)S(1)} %copy.38, bf16[800,1600]{1,0:T(8,128)(2,1)S(1)} %multiply_bitcast_fusion), kind=kLoop, calls=%fused_computation.3 | loop fusion | flops 7756800 | bytes 5150400 | tf_op jit(solution)/shard_map/concatenate | solution.py:337
  76.8 0.2 copy.39
  77.0 0.1 multiply_bitcast_fusion.1
  77.1 1.0 fusion.3.w3
  78.1 0.1 copy.40
  78.2 0.7 fusion.10.w4
  78.9 8.3 %chem.1 = (f32[3,8,32,8,128]{4,3,2,1,0:T(8,128)}, f32[8,128]{1,0:T(8,128)}) custom-call(s32[96]{0:T(128)} %bitcast.29, s32[96]{0:T(128)} %bitcast.30, f32[3,8,32,8,128]{4,3,2,1,0:T(8,128)} %flow.1.q_ref, bf16[1600,32]{1,0:T(8,128)(2,1)} %copy.41.w1, bf16[800,1616]{1,0:T(8,128)(2,1)} %fusion.1.w2, bf16[400,816]{1,0:T(8,128)(2,1)} %fusion.3.w3, ...), custom_call_target="tpu_custom_call" | custom-call | tf_op jit(solution)/shard_map/chem/pallas_call | solution.py:389
  87.1 0.1 broadcast_in_dim.7
  87.2 0.7 broadcast_in_dim.8.d_ref
  87.9 79.4 %diffuse.1 = (f32[3,8,32,8,128]{4,3,2,1,0:T(8,128)}, f32[8,128]{1,0:T(8,128)}) custom-call(f32[3,8,32,8,128]{4,3,2,1,0:T(8,128)} %get-tuple-element.6.q_ref, f32[3,8,128]{2,1,0:T(8,128)} %broadcast_in_dim.8.d_ref, f32[8,128]{1,0:T(8,128)} %get-tuple-element.7.act_in), custom_call_target="tpu_custom_call" | custom-call | tf_op jit(solution)/shard_map/diffuse/pallas_call | solution.py:408
  167.3 4.1 %copy.42 = f32[3,8,8,32,128]{4,3,2,1,0:T(8,128)} copy(f32[3,8,8,32,128]{4,1,3,2,0:T(8,128)} %bitcast.27) | data formatting | bytes 6291456 | tf_op jit(solution)/shard_map/transpose | solution.py:426
  171.4 1.2 slice.3
  (34 shorter events, 0.2 us)
Async XLA Ops:
  0.6 6.3 %copy-start.2 = (f32[3,8,32,128]{3,2,1,0:T(8,128)S(1)}, f32[3,8,32,128]{3,2,1,0:T(8,128)}, u32[]{:S(2)}) copy-start(f32[3,8,32,128]{3,2,1,0:T(8,128)} %param.14) | copy-start | bytes 1179652
  8.3 64.9 %copy-start.5 = (f32[1600]{0:T(1024)S(1)}, f32[1600]{0:T(1024)}, u32[]{:S(2)}) copy-start(f32[1600]{0:T(1024)} %param.17) | copy-start | bytes 19204
  8.3 65.0 %copy-start.3 = (bf16[24,1600]{1,0:T(8,128)(2,1)S(1)}, bf16[24,1600]{1,0:T(8,128)(2,1)}, u32[]{:S(2)}) copy-start(bf16[24,1600]{1,0:T(8,128)(2,1)} %param.16) | copy-start | bytes 230404
  8.3 66.0 %copy-start.6 = (f32[800]{0:T(1024)S(1)}, f32[800]{0:T(1024)}, u32[]{:S(2)}) copy-start(f32[800]{0:T(1024)} %param.19) | copy-start | bytes 9604
  8.3 66.3 %copy-start = (bf16[1600,800]{0,1:T(8,128)(2,1)S(1)}, bf16[1600,800]{0,1:T(8,128)(2,1)}, u32[]{:S(2)}) copy-start(bf16[1600,800]{0,1:T(8,128)(2,1)} %param.18) | copy-start | bytes 7680004
  74.9 1.8 %copy-start.7 = (f32[400]{0:T(512)S(1)}, f32[400]{0:T(512)}, u32[]{:S(2)}) copy-start(f32[400]{0:T(512)} %param.21) | copy-start | bytes 4804
  74.9 2.1 %copy-start.1 = (bf16[800,400]{0,1:T(8,128)(2,1)S(1)}, bf16[800,400]{0,1:T(8,128)(2,1)}, u32[]{:S(2)}) copy-start(bf16[800,400]{0,1:T(8,128)(2,1)} %param.20) | copy-start | bytes 1920004
  76.8 1.3 copy-start.9
  76.8 1.4 copy-start.4
  78.9 8.3 %copy-start.8 = (f32[24]{0:T(128)S(1)}, f32[24]{0:T(128)}, u32[]{:S(2)}) copy-start(f32[24]{0:T(128)} %param.15) | copy-start | bytes 292
where the time goes:
time: 173 us
  Pallas kernels  153 us (88%)
  local copies, waits for them, and re-layouts  15.2 us (9%)
  other arithmetic  3.95 us (2%)
    pallas_call x1, Pallas kernels, local(): pl.pallas_call(functools.partial(diffuse_kernel, chunks, cx, cy), out_sha...  79.4 us
    pallas_call x1, Pallas kernels, local(): pl.pallas_call(functools.partial(flow_kernel, chunks, cx, cy), out_shape=...  64.9 us
    pallas_call x1, Pallas kernels, local(): pl.pallas_call(functools.partial(chem_kernel, chunks, cy, group), out_sha...  8.26 us
    reshape x1, local copies, waits for them, and re-layouts, local(): q = fields.reshape(chunks, SUB, cx, cy, cz).transpose(0, 2, 3, 1, 4)  6.32 us
    transpose x1, local copies, waits for them, and re-layouts, local(): updated = updated.transpose(0, 3, 1, 2, 4).reshape(nf, cx, cy, cz)  4.09 us
    concatenate x4, other arithmetic, folded(): return jnp.concatenate([weight.T * jnp.bfloat16(scale), cols], axis=1)  3.48 us

commit v1 on v0

v1 whole, which is shorter than its diff:
```python
import functools

import jax
import jax.numpy as jnp
from jax import lax
from jax.experimental import pallas as pl
from jax.experimental.pallas import tpu as pltpu
from jax.sharding import PartitionSpec as P

AXES = ("gx", "gy", "gz")
MESH = pl.DeviceIdType.MESH
SUB = 8
LANES = 128
MIB = 1024 * 1024


def neighbours():
    ids = {a: lax.axis_index(a) for a in AXES}
    out = []
    for a in AXES:
        n = lax.axis_size(a)
        up = dict(ids)
        up[a] = lax.rem(ids[a] + 1, n)
        down = dict(ids)
        down[a] = lax.rem(ids[a] + n - 1, n)
        out.append((tuple(up[b] for b in AXES), tuple(down[b] for b in AXES)))
    return out


def enter(targets):
    barrier = pltpu.get_barrier_semaphore()
    for to in targets:
        pl.semaphore_signal(barrier, inc=1, device_id=to, device_id_type=MESH)
    pl.semaphore_wait(barrier, len(targets))


def peers(axis):
    ids = {a: lax.axis_index(a) for a in AXES}
    n = lax.axis_size(axis)
    out = []
    for k in range(1, n):
        to = dict(ids)
        to[axis] = lax.rem(ids[axis] + k, n)
        out.append(tuple(to[b] for b in AXES))
    return out


def remote(src, dst, send, recv, to):
    return pltpu.make_async_remote_copy(
        src_ref=src, dst_ref=dst, send_sem=send, recv_sem=recv,
        device_id=to, device_id_type=MESH)


def lane_ids():
    return lax.broadcasted_iota(jnp.int32, (SUB, LANES), 1)


class Grid:
    def __init__(self, cx, cy):
        self.cx, self.cy = cx, cy
        self.px, self.py = cx + 2, cy + 2 * SUB
        self.groups = cy // SUB

    def row(self, f, x, y=0):
        return (f * self.px + x + 1) * self.py + SUB + y

    def tile(self, f, x, g):
        r = (f * self.px + x + 1) * self.py + SUB + g * SUB
        return r if isinstance(r, int) else pl.multiple_of(r, SUB)


class Halo:
    def __init__(self, grid, width, near, xs, xr, ys, yr, zs, zr, send_sem, recv_sem):
        self.grid, self.width, self.near = grid, width, near
        self.xs, self.xr, self.ys, self.yr = xs, xr, ys, yr
        self.zs, self.zr, self.send_sem, self.recv_sem = zs, zr, send_sem, recv_sem
        lane = lane_ids()
        self.first, self.last = lane == 0, lane == LANES - 1
        self.even = lax.rem(lane, 2) == 0
        self.pair = lax.rem(lane + 1, LANES) // 2

    def copies(self, slot):
        (xu, xd), (yu, yd), (zu, zd) = self.near
        plan = [
            (self.xs.at[slot, 1], self.xr.at[slot, 0], xu),
            (self.xs.at[slot, 0], self.xr.at[slot, 1], xd),
            (self.ys.at[slot, 1], self.yr.at[slot, 0], yu),
            (self.ys.at[slot, 0], self.yr.at[slot, 1], yd),
            (self.zs.at[slot], self.zr.at[slot, 0], zu),
        ]
        if lax.axis_size("gz") > 2:
            plan.append((self.zs.at[slot], self.zr.at[slot, 1], zd))
        return [
            remote(s, d, self.send_sem.at[slot, i], self.recv_sem.at[slot, i], to)
            for i, (s, d, to) in enumerate(plan)
        ]

    def pack_z(self, face, t, k):
        return jnp.where(self.pair == k, pltpu.roll(t, 2 * k, 1) if k else t, face)

    def z_row(self, slot, x):
        if lax.axis_size("gz") > 2:
            return jnp.where(self.even, self.zr[slot, 1, x], self.zr[slot, 0, x])
        return self.zr[slot, 0, x]

    def z_near(self, t, zrow, k):
        r = pltpu.roll(zrow, LANES - 2 * k, 1) if k else zrow
        after = pltpu.roll(jnp.where(self.first, r, t), LANES - 1, 1)
        before = pltpu.roll(jnp.where(self.last, r, t), 1, 1)
        return after, before

    def send(self, slot, u, base):
        grid = self.grid
        for f in range(self.width):
            for side, x in ((0, 0), (1, grid.cx - 1)):
                self.xs[slot, side, f] = u[
                    pl.ds(grid.tile(base + f, x, 0), grid.cy), :].astype(jnp.bfloat16)
            for side, y in ((0, 0), (1, grid.cy - 1)):
                self.ys[slot, side, f] = u[
                    pl.ds(grid.row(base + f, 0, y), grid.cx, stride=grid.py), :]
        for c in self.copies(slot):
            c.start()

    def load_z(self, slot, u, base):
        grid = self.grid

        def body(x, _):
            face = jnp.zeros((SUB, LANES), jnp.float32)
            for g in range(grid.groups):
                for f in range(self.width):
                    t = u[pl.ds(grid.tile(base + f, x, g), SUB), :]
                    face = self.pack_z(face, t, f * grid.groups + g)
            self.zs[slot, x] = face
            return 0

        lax.fori_loop(0, grid.cx, body, 0)

    def receive(self, slot, u, base):
        grid = self.grid
        for c in self.copies(slot):
            c.wait_recv()
        for f in range(self.width):
            for side, x in ((0, -1), (1, grid.cx)):
                u[pl.ds(grid.tile(base + f, x, 0), grid.cy), :] = self.xr[
                    slot, side, f].astype(jnp.float32)
            for side, y in ((0, -1), (1, grid.cy)):
                u[pl.ds(grid.row(base + f, 0, y), grid.cx, stride=grid.py), :] = self.yr[
                    slot, side, f]

    def finish(self, slot):
        for c in self.copies(slot):
            c.wait_send()


def flow_kernel(nf, cx, cy, q_hbm, v_hbm, out_hbm, u_ref, w_ref, flow_ref, coef,
                vx, vy, vz, vys, vzs, xs, xr, ys, yr, zs, zr,
                send_sem, recv_sem, vs_sem, vr_sem, in_sem, out_sem):
    grid = Grid(cx, cy)
    chunks = nf // SUB
    loads = [pltpu.make_async_copy(
        v_hbm, w_ref.at[:, pl.ds(1, cx), pl.ds(SUB, cy)], in_sem.at[chunks])]
    for c in range(chunks):
        loads.append(pltpu.make_async_copy(
            q_hbm.at[pl.ds(c * SUB, SUB)],
            u_ref.at[0, pl.ds(c * SUB, SUB), pl.ds(1, cx), pl.ds(SUB, cy)], in_sem.at[c]))
    for copy in loads:
        copy.start()
    near = neighbours()
    (xu, xd), (yu, yd), (zu, zd) = near
    halo = Halo(grid, SUB, near, xs, xr, ys, yr, zs, zr, send_sem, recv_sem)
    rows = nf * grid.px * grid.py
    u2 = u_ref.reshape(3 * rows, LANES)
    w2 = w_ref.reshape(3 * grid.px * grid.py, LANES)
    enter([to for pair in near for to in pair])

    loads[0].wait()
    for side, y in ((0, 0), (1, cy - 1)):
        vys[side] = w2[pl.ds(grid.row(1, 0, y), cx, stride=grid.py), :]

    def pack_v(x, _):
        face = jnp.zeros((SUB, LANES), jnp.float32)
        for g in range(grid.groups):
            face = halo.pack_z(face, w2[pl.ds(grid.tile(2, x, g), SUB), :], g)
        vzs[x] = face
        return 0

    lax.fori_loop(0, cx, pack_v, 0)
    plan = [
        (w_ref.at[0, cx, pl.ds(SUB, cy)], vx.at[0], xu),
        (w_ref.at[0, 1, pl.ds(SUB, cy)], vx.at[1], xd),
        (vys.at[1], vy.at[0], yu),
        (vys.at[0], vy.at[1], yd),
        (vzs, vz.at[0], zu),
    ]
    if lax.axis_size("gz") > 2:
        plan.append((vzs, vz.at[1], zd))
    v_copies = [remote(s, d, vs_sem.at[i], vr_sem.at[i], to)
                for i, (s, d, to) in enumerate(plan)]
    for copy in v_copies:
        copy.start()
    for c in range(chunks):
        loads[1 + c].wait()
        halo.load_z(c, u2, c * SUB)
        halo.send(c, u2, c * SUB)

    for copy in v_copies:
        copy.wait_recv()
    for side, x in ((0, -1), (1, cx)):
        w2[pl.ds(grid.tile(0, x, 0), cy), :] = vx[side]
    for side, y in ((0, -1), (1, cy)):
        w2[pl.ds(grid.row(1, 0, y), cx, stride=grid.py), :] = vy[side]

    def make_coef(x, _):
        if lax.axis_size("gz") > 2:
            zrow = jnp.where(halo.even, vz[1, x], vz[0, x])
        else:
            zrow = vz[0, x]
        for g in range(grid.groups):
            r0 = grid.tile(0, x, g)
            r1 = grid.tile(1, x, g)
            after, before = halo.z_near(w2[pl.ds(grid.tile(2, x, g), SUB), :], zrow, g)
            values = (
                0.05 - 0.5 * w2[pl.ds(r0 + grid.py, SUB), :],
                0.05 + 0.5 * w2[pl.ds(r0 - grid.py, SUB), :],
                0.05 - 0.5 * w2[pl.ds(r1 + 1, SUB), :],
                0.05 + 0.5 * w2[pl.ds(r1 - 1, SUB), :],
                0.05 - 0.5 * after,
                0.05 + 0.5 * before,
            )
            for i, value in enumerate(values):
                coef[i, x, g] = value
        return 0

    lax.fori_loop(0, cx, make_coef, 0)

    def stencil(zrow, ks, row, k):
        t = u2[pl.ds(row, SUB), :]
        za, zb = halo.z_near(t, zrow, k)
        s = ks[0] * u2[pl.ds(row + grid.py, SUB), :] + ks[1] * u2[pl.ds(row - grid.py, SUB), :]
        s = s + (ks[2] * u2[pl.ds(row + 1, SUB), :] + ks[3] * u2[pl.ds(row - 1, SUB), :])
        return t, s + (ks[4] * za + ks[5] * zb)

    stores = []
    for stage in range(3):
        weight = (1.0 / 3.0, 0.5, 1.0)[stage]
        for c in range(chunks):
            slot = stage * chunks + c
            first = stage * nf + c * SUB
            halo.receive(slot, u2, first)

            def body(x, _):
                zrow = halo.z_row(slot, x)
                face = jnp.zeros((SUB, LANES), jnp.float32)
                for g in range(grid.groups):
                    ks = [coef[i, x, g] for i in range(6)]
                    for f in range(SUB):
                        k = f * grid.groups + g
                        t, s = stencil(zrow, ks, grid.tile(first + f, x, g), k)
                        q = u2[pl.ds(grid.tile(c * SUB + f, x, g), SUB), :]
                        r = q + weight * (s - 0.3 * t)
                        if stage == 2:
                            flow_ref[c * SUB + f, x, pl.ds(g * SUB, SUB)] = r
                        else:
                            u2[pl.ds(grid.tile(first + nf + f, x, g), SUB), :] = r
                            face = halo.pack_z(face, r, k)
                if stage < 2:
                    zs[slot + chunks, x] = face
                return 0

            lax.fori_loop(0, cx, body, 0)
            if stage < 2:
                halo.send(slot + chunks, u2, first + nf)
            else:
                part = pl.ds(c * SUB, SUB)
                stores.append(pltpu.make_async_copy(
                    flow_ref.at[part], out_hbm.at[part], out_sem.at[c]))
                stores[-1].start()
    for copy in v_copies:
        copy.wait_send()
    for slot in range(3 * chunks):
        halo.finish(slot)
    for copy in stores:
        copy.wait()


def diffuse_kernel(nf, cx, cy, d_ref, q_hbm, act_in, out_hbm, act_out, u_ref, new_ref, part,
                   got, act_send, act_recv, xs, xr, ys, yr, zs, zr, send_sem, recv_sem,
                   in_sem, out_sem):
    grid = Grid(cx, cy)
    chunks = nf // SUB
    loads = []
    for c in range(chunks):
        loads.append(pltpu.make_async_copy(
            q_hbm.at[pl.ds(c * SUB, SUB)],
            u_ref.at[pl.ds(c * SUB, SUB), pl.ds(1, cx), pl.ds(SUB, cy)], in_sem.at[c]))
        loads[-1].start()
    near = neighbours()
    groups = [peers(a) for a in AXES[::-1]]
    enter([to for g in groups for to in g])
    halo = Halo(grid, SUB, near, xs, xr, ys, yr, zs, zr, send_sem, recv_sem)
    lane = lane_ids()
    u2 = u_ref.reshape(nf * grid.px * grid.py, LANES)

    def hops(phase):
        return [remote(part.at[phase], got.at[phase, k], act_send.at[phase, k],
                       act_recv.at[phase, k], to)
                for k, to in enumerate(groups[phase])]

    def gather(phase):
        for h in hops(phase):
            h.wait_recv()
        total = part[phase]
        for k in range(len(groups[phase])):
            total = total + got[phase, k]
        return total

    part[0] = act_in[...]
    for c in range(chunks):
        loads[c].wait()
        halo.load_z(c, u2, c * SUB)
        halo.send(c, u2, c * SUB)
        if c == 0:
            for h in hops(0):
                h.start()
    stores = []
    for c in range(chunks):
        if c < len(groups) - 1:
            part[c + 1] = gather(c)
            for h in hops(c + 1):
                h.start()
        first = c * SUB
        halo.receive(c, u2, first)

        def body(x, _):
            zrow = halo.z_row(c, x)
            for f in range(SUB):
                rate = d_ref[first + f]
                for g in range(grid.groups):
                    row = grid.tile(first + f, x, g)
                    t = u2[pl.ds(row, SUB), :]
                    za, zb = halo.z_near(t, zrow, f * grid.groups + g)
                    s = u2[pl.ds(row + grid.py, SUB), :] + u2[pl.ds(row - grid.py, SUB), :]
                    s = s + (u2[pl.ds(row + 1, SUB), :] + u2[pl.ds(row - 1, SUB), :])
                    s = s + (za + zb)
                    new_ref[first + f, x, pl.ds(g * SUB, SUB)] = t + rate * (s - 6.0 * t)
            return 0

        lax.fori_loop(0, cx, body, 0)
        chunk = pl.ds(first, SUB)
        stores.append(pltpu.make_async_copy(new_ref.at[chunk], out_hbm.at[chunk], out_sem.at[c]))
        stores[-1].start()
    done = min(chunks, len(groups) - 1)
    for phase in range(done, len(groups) - 1):
        part[phase + 1] = gather(phase)
        for h in hops(phase + 1):
            h.start()
    total = gather(len(groups) - 1)
    me = (lax.axis_index("gx") * lax.axis_size("gy") + lax.axis_index("gy")) * lax.axis_size(
        "gz") + lax.axis_index("gz")
    flat = lax.broadcasted_iota(jnp.int32, (SUB, LANES), 0) * LANES + lane
    act_out[0] = jnp.sum(jnp.where(flat == me, total, 0.0))
    for phase in range(len(groups)):
        for h in hops(phase):
            h.wait_send()
    for c in range(chunks):
        halo.finish(c)
    for copy in stores:
        copy.wait()


def widen(dst, weight, scale, cols):
    k = weight.shape[1]
    dst[:, :k] = weight[...] * jnp.bfloat16(scale)
    dst[:, k:] = cols


def chem_kernel(nf, cells, group, list_ref, owner_ref, q_ref, w1, w2_in, w3_in, w4_in, cols,
                out_ref, act_ref, w2, w3, w4, x_in, h1, h2, h3, inc):
    listed = list_ref.shape[0]
    n_lanes = group * LANES
    chunks = nf // SUB
    out_ref[...] = q_ref[...]
    act_ref[...] = jnp.zeros_like(act_ref)
    n2, n3, n4 = w2.shape[0], w3.shape[0], w4.shape[0]
    widen(w2, w2_in, 0.5, cols[:n2])
    widen(w3, w3_in, 0.5, cols[n2:n2 + n3])
    widen(w4, w4_in, 1.0, cols[n2 + n3:])
    flat = (lax.broadcasted_iota(jnp.int32, (SUB, LANES), 0) * LANES + lane_ids())
    row = lax.broadcasted_iota(jnp.int32, (16, n_lanes), 0)
    ones = jnp.where(row < 3, 1.0, 0.0)
    x_in[nf:nf + SUB] = ones[:SUB]
    for h in (h1, h2, h3):
        h[h.shape[0] - 16:] = ones.astype(jnp.bfloat16)
    count = lax.fori_loop(
        0, listed, lambda i, n: n + jnp.where(list_ref[i] >= 0, 1, 0), 0)

    def layer(w, src, dst, step):
        rows = w.shape[0]
        for m in range(0, rows, step):
            k = min(step, rows - m)
            h = jnp.dot(w[m:m + k], src, preferred_element_type=jnp.float32)
            dst[m:m + k] = (h + h * jnp.tanh(h)).astype(jnp.bfloat16)

    def run(g, _):
        base = g * group
        for i in range(group):
            b = jnp.maximum(list_ref[base + i], 0)
            for c in range(chunks):
                x_in[c * SUB:(c + 1) * SUB, i * LANES:(i + 1) * LANES] = q_ref[
                    pl.ds(c * SUB * cells + b, SUB, stride=cells), :]
        layer(w1, x_in[...].astype(jnp.bfloat16), h1, 400)
        layer(w2, h1[...], h2, 400)
        layer(w3, h2[...], h3, 400)
        inc[...] = jnp.dot(w4[...], h3[...], preferred_element_type=jnp.float32)
        for i in range(group):
            entry = list_ref[base + i]
            b = jnp.maximum(entry, 0)
            valid = jnp.where(entry >= 0, 1.0, 0.0)
            for c in range(chunks):
                t = inc[c * SUB:(c + 1) * SUB, i * LANES:(i + 1) * LANES]
                where = pl.ds(c * SUB * cells + b, SUB, stride=cells)
                out_ref[where, :] = out_ref[where, :] + valid * t
            r = inc[0:1, i * LANES:(i + 1) * LANES]
            heat = jnp.sum(r * r, axis=1, keepdims=True) * (valid / (8.0 * LANES))
            act_ref[...] = act_ref[...] + jnp.where(flat == owner_ref[base + i], heat, 0.0)
        return 0

    lax.fori_loop(0, (count + group - 1) // group, run, 0)


def bias_columns(bias, width):
    rest = bias
    parts = []
    for _ in range(3):
        part = lax.reduce_precision(rest, 8, 7)
        rest = rest - part
        parts.append(part)
    lane = lax.broadcasted_iota(jnp.int32, (bias.shape[0], width), 1)
    out = jnp.zeros((bias.shape[0], width), jnp.float32)
    for i, part in enumerate(parts):
        out = jnp.where(lane == i, part[:, None], out)
    return out.astype(jnp.bfloat16)


def halo_scratch(slots, cx, cy):
    return [
        pltpu.VMEM((slots, 2, SUB, cy, LANES), jnp.bfloat16),
        pltpu.VMEM((slots, 2, SUB, cy, LANES), jnp.bfloat16),
        pltpu.VMEM((slots, 2, SUB, cx, LANES), jnp.float32),
        pltpu.VMEM((slots, 2, SUB, cx, LANES), jnp.float32),
        pltpu.VMEM((slots, cx, SUB, LANES), jnp.float32),
        pltpu.VMEM((slots, 2, cx, SUB, LANES), jnp.float32),
        pltpu.SemaphoreType.DMA((slots, 6)),
        pltpu.SemaphoreType.DMA((slots, 6)),
    ]


def spec(space, n=1):
    return [pl.BlockSpec(memory_space=space)] * n


def local(fields, velocity, diffusivity, weight_in, bias_in, weight_mid, bias_mid,
          weight_low, bias_low, weight_out, bias_out, react_list, owner_table):
    nf, cx, cy, cz = fields.shape
    chunks = nf // SUB
    cells = cx * cy
    padded = (cx + 2, cy + 2 * SUB, cz)
    slots = 3 * chunks
    dma = pltpu.SemaphoreType.DMA
    halos = halo_scratch(slots, cx, cy)
    flowed = pl.pallas_call(
        functools.partial(flow_kernel, nf, cx, cy),
        out_shape=jax.ShapeDtypeStruct(fields.shape, jnp.float32),
        in_specs=spec(pl.ANY, 2),
        out_specs=spec(pl.ANY)[0],
        scratch_shapes=[
            pltpu.VMEM((3, nf) + padded, jnp.float32),
            pltpu.VMEM((3,) + padded, jnp.float32),
            pltpu.VMEM((nf, cx, cy, cz), jnp.float32),
            pltpu.VMEM((6, cx, cy // SUB, SUB, cz), jnp.float32),
            pltpu.VMEM((2, cy, cz), jnp.float32),
            pltpu.VMEM((2, cx, cz), jnp.float32),
            pltpu.VMEM((2, cx, SUB, cz), jnp.float32),
            pltpu.VMEM((2, cx, cz), jnp.float32),
            pltpu.VMEM((cx, SUB, cz), jnp.float32),
        ] + halos + [dma((6,)), dma((6,)), dma((chunks + 1,)), dma((chunks,))],
        compiler_params=pltpu.CompilerParams(
            collective_id=0, has_side_effects=True, vmem_limit_bytes=40 * MIB),
        name="flow",
    )(fields, velocity)

    group = 4
    h = (weight_in.shape[1], weight_mid.shape[1], weight_low.shape[1])
    half = jnp.bfloat16(0.5)
    w1 = jnp.concatenate([weight_in.T * half, bias_columns(bias_in * 0.5, SUB)], axis=1)
    cols = bias_columns(
        jnp.concatenate([bias_mid * 0.5, bias_low * 0.5, bias_out]), 16)
    n_lanes = group * LANES
    reacted, activity = pl.pallas_call(
        functools.partial(chem_kernel, nf, cells, group),
        out_shape=(jax.ShapeDtypeStruct((nf * cells, cz), jnp.float32),
                   jax.ShapeDtypeStruct((SUB, LANES), jnp.float32)),
        in_specs=spec(pltpu.SMEM, 2) + spec(pltpu.VMEM, 6),
        out_specs=tuple(spec(pltpu.VMEM, 2)),
        scratch_shapes=[
            pltpu.VMEM((h[1], h[0] + 16), jnp.bfloat16),
            pltpu.VMEM((h[2], h[1] + 16), jnp.bfloat16),
            pltpu.VMEM((nf, h[2] + 16), jnp.bfloat16),
            pltpu.VMEM((nf + SUB, n_lanes), jnp.float32),
            pltpu.VMEM((h[0] + 16, n_lanes), jnp.bfloat16),
            pltpu.VMEM((h[1] + 16, n_lanes), jnp.bfloat16),
            pltpu.VMEM((h[2] + 16, n_lanes), jnp.bfloat16),
            pltpu.VMEM((nf, n_lanes), jnp.float32),
        ],
        compiler_params=pltpu.CompilerParams(vmem_limit_bytes=40 * MIB),
        name="chem",
    )(react_list[0], owner_table[0], flowed.reshape(nf * cells, cz), w1,
      weight_mid.T, weight_low.T, weight_out.T, cols)

    most = max(lax.axis_size(a) for a in AXES) - 1
    updated, mine = pl.pallas_call(
        functools.partial(diffuse_kernel, nf, cx, cy),
        out_shape=(jax.ShapeDtypeStruct(fields.shape, jnp.float32),
                   jax.ShapeDtypeStruct((1,), jnp.float32)),
        in_specs=spec(pltpu.SMEM) + spec(pl.ANY) + spec(pltpu.VMEM),
        out_specs=(spec(pl.ANY)[0], spec(pltpu.SMEM)[0]),
        scratch_shapes=[
            pltpu.VMEM((nf,) + padded, jnp.float32),
            pltpu.VMEM((nf, cx, cy, cz), jnp.float32),
            pltpu.VMEM((len(AXES), SUB, LANES), jnp.float32),
            pltpu.VMEM((len(AXES), most, SUB, LANES), jnp.float32),
            dma((len(AXES), most)),
            dma((len(AXES), most)),
        ] + halo_scratch(chunks, cx, cy) + [dma((chunks,)), dma((chunks,))],
        compiler_params=pltpu.CompilerParams(
            collective_id=1, has_side_effects=True, vmem_limit_bytes=40 * MIB),
        name="diffuse",
    )(diffusivity, reacted.reshape(fields.shape), activity)
    return updated, mine


def solution(mesh):
    return jax.shard_map(
        local,
        mesh=mesh,
        in_specs=(P(None, *AXES), P(None, *AXES)) + (P(),) * 9
        + (P(AXES, None), P(AXES, None)),
        out_specs=(P(None, *AXES), P(AXES)),
        check_vma=False,
    )
```

time: 173 us -> 160 us (0.925)
  local copies, waits for them, and re-layouts: 15.2 us -> 5.56 us
  Pallas kernels: 153 us -> 147 us
    reshape x1 -> x0, local copies, waits for them, and re-layouts: 6.32 us -> none  [local(): q = fields.reshape(chunks, SUB, cx, cy, cz).transpose(0, 2, 3, 1, 4)]
    pallas_call x3, Pallas kernels: 153 us -> 147 us  [the longest x1 78.1 us: local(): pl.pallas_call(functools.partial(diffuse_kernel, nf, cx, cy), out_shape=(...]
    transpose x2 -> x0, local copies, waits for them, and re-layouts: 5.17 us -> none  [the longest x1 4.09 us: local(): updated = updated.transpose(0, 3, 1, 2, 4).reshape(nf, cx, cy, cz)]
    unnamed x21 -> x17, local copies, waits for them, and re-layouts: 0.32 us -> 4.58 us
    concatenate x4 -> x1, other arithmetic: 3.48 us -> 0.01 us  [local(): jnp.concatenate([weight_in.T * half, bias_columns(bias_in * 0.5, SUB)], a...]
    mul x3, other arithmetic: 0.36 us -> 2.27 us  [the longest x1 0.9 us: local(): weight_in.T * half]
where the time goes in v1:
time: 160 us; the launch traced here: 159 us
  Pallas kernels  147 us (92%)
  local copies, waits for them, and re-layouts  5.56 us (3%)
  other arithmetic  3.65 us (2%)
  between operations  2.47 us (2%)
    pallas_call x1, Pallas kernels, local(): pl.pallas_call(functools.partial(diffuse_kernel, nf, cx, cy), out_shape=(...  78.1 us
    pallas_call x1, Pallas kernels, local(): pl.pallas_call(functools.partial(flow_kernel, nf, cx, cy), out_shape=jax....  64.5 us
    unnamed x17, local copies, waits for them, and re-layouts  4.58 us
    pallas_call x1, Pallas kernels, local(): pl.pallas_call(functools.partial(chem_kernel, nf, cells, group), out_shap...  4.5 us

profile of v1, /device:TPU:0, one launch (start us, length us, event | category | flops | bytes accessed | tf_op | source)
XLA Modules:
  0.0 158.8 jit_solution(11035417281355659629)
XLA Ops:
  0.7 0.7 broadcast_multiply_fusion.1
  1.4 0.7 broadcast_multiply_fusion
  2.1 0.7 concatenate.22
  2.8 0.7 subtract_reduce-precision_fusion.1
  3.5 0.1 select_convert_fusion.1
  3.6 0.9 multiply_bitcast_fusion
  4.5 0.6 select_convert_fusion.cols
  5.1 0.3 copy.16.w1
  5.3 0.0 copy-start
  5.3 1.9 %copy-done = f32[24,8,32,128]{3,2,1,0:T(8,128)S(1)} copy-done((f32[24,8,32,128]{3,2,1,0:T(8,128)S(1)}, f32[24,8,32,128]{3,2,1,0:T(8,128)}, u32[]{:S(2)}) %copy-start) | copy-done | bytes 3145752
  7.2 0.0 copy-start.3
  7.2 1.0 copy-done.3
  8.2 0.0 copy-start.6
  8.2 64.5 %flow.1 = f32[24,8,32,128]{3,2,1,0:T(8,128)S(1)} custom-call(f32[24,8,32,128]{3,2,1,0:T(8,128)S(1)} %copy-done, f32[3,8,32,128]{3,2,1,0:T(8,128)S(1)} %copy-done.3), custom_call_target="tpu_custom_call" | custom-call | tf_op jit(solution)/shard_map/flow/pallas_call | solution.py:471
  72.7 0.0 copy-done.1
  72.7 0.0 copy-done.2
  72.7 0.0 copy-done.4
  72.7 0.0 copy-done.5
  72.8 0.0 copy-done.6
  72.8 0.0 copy-start.7
  72.8 4.5 %chem.1 = (f32[6144,128]{1,0:T(8,128)S(1)}, f32[8,128]{1,0:T(8,128)S(1)}) custom-call(s32[96]{0:T(128)S(1)} %bitcast.14, s32[96]{0:T(128)S(1)} %bitcast.15, f32[6144,128]{1,0:T(8,128)S(1)} %bitcast.9, bf16[1600,32]{1,0:T(8,128)(2,1)S(1)} %copy.16.w1, bf16[800,1600]{1,0:T(8,128)(2,1)S(1)} %bitcast.11, bf16[400,800]{1,0:T(8,128)(2,1)S(1)} %bitcast.12, ...), custom_call_target="tpu_custom_call" | custom-call | tf_op jit(solution)/shard_map/chem/pallas_call | solution.py:499
  77.3 0.0 copy-done.7
  77.3 78.1 %diffuse.1 = (f32[24,8,32,128]{3,2,1,0:T(8,128)S(1)}, f32[1]{0:T(128)}) custom-call(f32[24]{0:T(128)S(1)} %copy-done.7, f32[24,8,32,128]{3,2,1,0:T(8,128)S(1)} %bitcast.10, f32[8,128]{1,0:T(8,128)S(1)} %get-tuple-element.5.act_in), custom_call_target="tpu_custom_call" | custom-call | tf_op jit(solution)/shard_map/diffuse/pallas_call | solution.py:521
  155.4 1.7 %copy.19 = f32[24,8,32,128]{3,2,1,0:T(8,128)} copy(f32[24,8,32,128]{3,2,1,0:T(8,128)S(1)} %get-tuple-element.18) | data formatting | bytes 6291456
  (10 shorter events, 0.1 us)
Async XLA Ops:
  5.3 1.9 %copy-start = (f32[24,8,32,128]{3,2,1,0:T(8,128)S(1)}, f32[24,8,32,128]{3,2,1,0:T(8,128)}, u32[]{:S(2)}) copy-start(f32[24,8,32,128]{3,2,1,0:T(8,128)} %q_hbm.1) | copy-start | bytes 9437188
  7.2 1.0 copy-start.3
  8.2 64.5 %copy-start.1 = (bf16[1600,800]{0,1:T(8,128)(2,1)S(1)}, bf16[1600,800]{0,1:T(8,128)(2,1)}, u32[]{:S(2)}) copy-start(bf16[1600,800]{0,1:T(8,128)(2,1)} %param.18) | copy-start | bytes 7680004
  8.2 64.5 %copy-start.2 = (bf16[800,400]{0,1:T(8,128)(2,1)S(1)}, bf16[800,400]{0,1:T(8,128)(2,1)}, u32[]{:S(2)}) copy-start(bf16[800,400]{0,1:T(8,128)(2,1)} %param.20) | copy-start | bytes 1920004
  8.2 64.5 %copy-start.4 = (bf16[400,24]{0,1:T(8,128)(2,1)S(1)}, bf16[400,24]{0,1:T(8,128)(2,1)}, u32[]{:S(2)}) copy-start(bf16[400,24]{0,1:T(8,128)(2,1)} %param.22) | copy-start | bytes 57604
  8.2 64.5 %copy-start.5 = (s32[1,96]{1,0:T(1,128)S(1)}, s32[1,96]{1,0:T(1,128)}, u32[]{:S(2)}) copy-start(s32[1,96]{1,0:T(1,128)} %param.24) | copy-start | bytes 1156
  8.2 64.5 %copy-start.6 = (s32[1,96]{1,0:T(1,128)S(1)}, s32[1,96]{1,0:T(1,128)}, u32[]{:S(2)}) copy-start(s32[1,96]{1,0:T(1,128)} %param.25) | copy-start | bytes 1156
  72.8 4.5 %copy-start.7 = (f32[24]{0:T(128)S(1)}, f32[24]{0:T(128)}, u32[]{:S(2)}) copy-start(f32[24]{0:T(128)} %d_ref.1) | copy-start | bytes 292

commit v2 on v1

v2 whole, which is shorter than its diff:
```python
import functools

import jax
import jax.numpy as jnp
from jax import lax
from jax.experimental import pallas as pl
from jax.experimental.pallas import tpu as pltpu
from jax.sharding import PartitionSpec as P

AXES = ("gx", "gy", "gz")
MESH = pl.DeviceIdType.MESH
SUB = 8
LANES = 128
MIB = 1024 * 1024


def neighbours():
    ids = {a: lax.axis_index(a) for a in AXES}
    out = []
    for a in AXES:
        n = lax.axis_size(a)
        up = dict(ids)
        up[a] = lax.rem(ids[a] + 1, n)
        down = dict(ids)
        down[a] = lax.rem(ids[a] + n - 1, n)
        out.append((tuple(up[b] for b in AXES), tuple(down[b] for b in AXES)))
    return out


def enter(targets):
    barrier = pltpu.get_barrier_semaphore()
    for to in targets:
        pl.semaphore_signal(barrier, inc=1, device_id=to, device_id_type=MESH)
    pl.semaphore_wait(barrier, len(targets))


def peers(axis):
    ids = {a: lax.axis_index(a) for a in AXES}
    n = lax.axis_size(axis)
    out = []
    for k in range(1, n):
        to = dict(ids)
        to[axis] = lax.rem(ids[axis] + k, n)
        out.append(tuple(to[b] for b in AXES))
    return out


def remote(src, dst, send, recv, to):
    return pltpu.make_async_remote_copy(
        src_ref=src, dst_ref=dst, send_sem=send, recv_sem=recv,
        device_id=to, device_id_type=MESH)


def lane_ids():
    return lax.broadcasted_iota(jnp.int32, (SUB, LANES), 1)


class Grid:
    def __init__(self, cx, cy):
        self.cx, self.cy = cx, cy
        self.px, self.py = cx + 2, cy + 2 * SUB
        self.groups = cy // SUB

    def row(self, f, x, y=0):
        return (f * self.px + x + 1) * self.py + SUB + y

    def tile(self, f, x, g):
        r = (f * self.px + x + 1) * self.py + SUB + g * SUB
        return r if isinstance(r, int) else pl.multiple_of(r, SUB)


class Halo:
    def __init__(self, grid, width, near, xs, xr, ys, yr, zs, zr, send_sem, recv_sem):
        self.grid, self.width, self.near = grid, width, near
        self.xs, self.xr, self.ys, self.yr = xs, xr, ys, yr
        self.zs, self.zr, self.send_sem, self.recv_sem = zs, zr, send_sem, recv_sem
        lane = lane_ids()
        self.first, self.last = lane == 0, lane == LANES - 1
        self.even = lax.rem(lane, 2) == 0
        self.pair = lax.rem(lane + 1, LANES) // 2

    def copies(self, slot):
        (xu, xd), (yu, yd), (zu, zd) = self.near
        plan = [
            (self.xs.at[slot, 1], self.xr.at[slot, 0], xu),
            (self.xs.at[slot, 0], self.xr.at[slot, 1], xd),
            (self.ys.at[slot, 1], self.yr.at[slot, 0], yu),
            (self.ys.at[slot, 0], self.yr.at[slot, 1], yd),
            (self.zs.at[slot], self.zr.at[slot, 0], zu),
        ]
        if lax.axis_size("gz") > 2:
            plan.append((self.zs.at[slot], self.zr.at[slot, 1], zd))
        return [
            remote(s, d, self.send_sem.at[slot, i], self.recv_sem.at[slot, i], to)
            for i, (s, d, to) in enumerate(plan)
        ]

    def pack_z(self, face, t, k):
        return jnp.where(self.pair == k, pltpu.roll(t, 2 * k, 1) if k else t, face)

    def z_row(self, slot, x):
        if lax.axis_size("gz") > 2:
            return jnp.where(self.even, self.zr[slot, 1, x], self.zr[slot, 0, x])
        return self.zr[slot, 0, x]

    def z_near(self, t, zrow, k):
        r = pltpu.roll(zrow, LANES - 2 * k, 1) if k else zrow
        after = pltpu.roll(jnp.where(self.first, r, t), LANES - 1, 1)
        before = pltpu.roll(jnp.where(self.last, r, t), 1, 1)
        return after, before

    def send(self, slot, u, base):
        grid = self.grid
        for f in range(self.width):
            for side, x in ((0, 0), (1, grid.cx - 1)):
                self.xs[slot, side, f] = u[
                    pl.ds(grid.tile(base + f, x, 0), grid.cy), :].astype(jnp.bfloat16)
            for side, y in ((0, 0), (1, grid.cy - 1)):
                self.ys[slot, side, f] = u[
                    pl.ds(grid.row(base + f, 0, y), grid.cx, stride=grid.py), :]
        for c in self.copies(slot):
            c.start()

    def load_z(self, slot, u, base):
        grid = self.grid

        def body(x, _):
            face = jnp.zeros((SUB, LANES), jnp.float32)
            for g in range(grid.groups):
                for f in range(self.width):
                    t = u[pl.ds(grid.tile(base + f, x, g), SUB), :]
                    face = self.pack_z(face, t, f * grid.groups + g)
            self.zs[slot, x] = face
            return 0

        lax.fori_loop(0, grid.cx, body, 0)

    def receive(self, slot, u, base):
        grid = self.grid
        for c in self.copies(slot):
            c.wait_recv()
        for f in range(self.width):
            for side, x in ((0, -1), (1, grid.cx)):
                u[pl.ds(grid.tile(base + f, x, 0), grid.cy), :] = self.xr[
                    slot, side, f].astype(jnp.float32)
            for side, y in ((0, -1), (1, grid.cy)):
                u[pl.ds(grid.row(base + f, 0, y), grid.cx, stride=grid.py), :] = self.yr[
                    slot, side, f]

    def finish(self, slot):
        for c in self.copies(slot):
            c.wait_send()


class Team:
    def __init__(self):
        self.nx, self.ny, self.nz = (lax.axis_size(a) for a in AXES)
        self.span = 2 if self.ny % 2 == 0 else self.ny
        self.size = self.nx * self.span * self.nz

    def slots(self, listed):
        return 2 * ((listed + 2 * self.size - 1) // (2 * self.size))

    def place(self):
        i, j, k = (lax.axis_index(a) for a in AXES)
        return (i * self.span + lax.rem(j, self.span)) * self.nz + k

    def member(self, step):
        m = lax.rem(self.place() + step, self.size)
        i = m // (self.span * self.nz)
        j = lax.rem(m // self.nz, self.span)
        j = j + (lax.axis_index("gy") // self.span) * self.span
        return (i, j, lax.rem(m, self.nz))


def bias_rows(dst, row, lane, bias, scale):
    n = bias.shape[0]
    rest = bias[...].reshape(1, n) * scale
    for i in range(3):
        part = rest.astype(jnp.bfloat16).astype(jnp.float32)
        rest = rest - part
        dst[row + i:row + i + 1, lane:lane + n] = part


def turned(dst, src):
    for j in range(0, src.shape[1], LANES):
        dst[j:j + LANES] = src[:, j:j + LANES].T.astype(jnp.bfloat16)


def widen(dst, src, scale, cols, first):
    rows, k = src.shape
    step = 16 if rows % 16 == 0 else rows

    def body(j, _):
        at = pl.ds(pl.multiple_of(j * step, step), step)
        dst[at, pl.ds(0, k)] = src[at, :] * jnp.bfloat16(scale)
        dst[at, pl.ds(k, 16)] = cols[pl.ds(pl.multiple_of(first + j * step, 8), step),
                                     pl.ds(0, 16)]
        return 0

    lax.fori_loop(0, rows // step, body, 0)


def up(n, m):
    return (n + m - 1) // m * m


def flow_kernel(nf, cx, cy, list_hbm, q_hbm, v_hbm, wi_hbm, wm_hbm, wl_hbm, wo_hbm,
                b1_hbm, b2_hbm, b3_hbm, b4_hbm,
                out_hbm, slot_hbm, count_hbm, rest_hbm, w1_hbm, w2_hbm, w3_hbm, w4_hbm,
                list_ref, u0, u1, u2, w_ref, flow_ref, coef, sd, rv, cs, cr,
                wi, wm, wl, wo, b1, b2, b3, b4, t1, t2, cols, w1, w2, w3, w4,
                h1, h2, h3, rest,
                vx, vy, vz, vys, vzs, xs, xr, ys, yr, zs, zr,
                send_sem, recv_sem, vs_sem, vr_sem, in_sem, out_sem,
                team_send, team_recv, w_in, w_out, back_sem):
    grid = Grid(cx, cy)
    chunks = nf // SUB
    cells = cx * cy
    team = Team()
    listed = list_ref.shape[1]
    loads = [pltpu.make_async_copy(
        v_hbm, w_ref.at[:, pl.ds(1, cx), pl.ds(SUB, cy)], in_sem.at[chunks])]
    for c in range(chunks):
        loads.append(pltpu.make_async_copy(
            q_hbm.at[pl.ds(c * SUB, SUB)],
            u0.at[pl.ds(c * SUB, SUB), pl.ds(1, cx), pl.ds(SUB, cy)], in_sem.at[c]))
    for i, (src, dst) in enumerate((
            (wi_hbm, wi), (b1_hbm, b1), (b2_hbm, b2), (b3_hbm, b3), (b4_hbm, b4),
            (wo_hbm, wo), (list_hbm, list_ref), (wl_hbm, wl), (wm_hbm, wm))):
        loads.append(pltpu.make_async_copy(src, dst, w_in.at[i]))
    for copy in loads:
        copy.start()
    w_loads = loads[1 + chunks:]
    near = neighbours()
    (xu, xd), (yu, yd), (zu, zd) = near
    halo = Halo(grid, SUB, near, xs, xr, ys, yr, zs, zr, send_sem, recv_sem)
    rows = nf * grid.px * grid.py
    us = [u.reshape(rows, LANES) for u in (u0, u1, u2)]
    vv = w_ref.reshape(3 * grid.px * grid.py, LANES)
    members = [team.member(k) for k in range(team.size)]
    enter([to for pair in near for to in pair] + members[1:])

    loads[0].wait()
    for side, y in ((0, 0), (1, cy - 1)):
        vys[side] = vv[pl.ds(grid.row(1, 0, y), cx, stride=grid.py), :]

    def pack_v(x, _):
        face = jnp.zeros((SUB, LANES), jnp.float32)
        for g in range(grid.groups):
            face = halo.pack_z(face, vv[pl.ds(grid.tile(2, x, g), SUB), :], g)
        vzs[x] = face
        return 0

    lax.fori_loop(0, cx, pack_v, 0)
    plan = [
        (w_ref.at[0, cx, pl.ds(SUB, cy)], vx.at[0], xu),
        (w_ref.at[0, 1, pl.ds(SUB, cy)], vx.at[1], xd),
        (vys.at[1], vy.at[0], yu),
        (vys.at[0], vy.at[1], yd),
        (vzs, vz.at[0], zu),
    ]
    if lax.axis_size("gz") > 2:
        plan.append((vzs, vz.at[1], zd))
    v_copies = [remote(s, d, vs_sem.at[i], vr_sem.at[i], to)
                for i, (s, d, to) in enumerate(plan)]
    for copy in v_copies:
        copy.start()
    for c in range(chunks):
        loads[1 + c].wait()
        halo.load_z(c, us[0], c * SUB)
        halo.send(c, us[0], c * SUB)

    for copy in w_loads:
        copy.wait()
    count = lax.fori_loop(
        0, listed, lambda i, n: n + jnp.where(list_ref[0, i] >= 0, 1, 0), 0)
    cs[...] = jnp.full((1, LANES), count, jnp.int32)
    cr[0] = cs[...]
    counts = [remote(cs, cr.at[k], team_send.at[chunks, k], team_recv.at[chunks, k], members[k])
              for k in range(1, team.size)]
    for copy in counts:
        copy.start()

    t1[...] = jnp.zeros_like(t1)
    t2[...] = jnp.zeros_like(t2)
    n2, n3 = up(w2.shape[0], LANES), up(w3.shape[0], LANES)
    t1[0:nf, 0:wi.shape[1]] = wi[...].astype(jnp.float32) * 0.5
    bias_rows(t1, nf, 0, b1, 0.5)
    bias_rows(t2, 0, 0, b2, 0.5)
    bias_rows(t2, 0, n2, b3, 0.5)
    bias_rows(t2, 0, n2 + n3, b4, 1.0)
    turned(w1, t1)
    turned(cols, t2)
    widen(w2, wm, 0.5, cols, 0)
    widen(w3, wl, 0.5, cols, n2)
    widen(w4, wo, 1.0, cols, n2 + n3)
    for h in (h1, h2, h3):
        h[h.shape[0] - 16:] = bias_ones(16, LANES).astype(jnp.bfloat16)
    origin = jnp.concatenate(
        [jnp.zeros((nf, LANES), jnp.float32), bias_ones(w1.shape[1] - nf, LANES)], axis=0)
    rest[...] = network(origin.astype(jnp.bfloat16), w1, w2, w3, w4, h1, h2, h3)
    stores = [pltpu.make_async_copy(src, dst, w_out.at[i]) for i, (src, dst) in enumerate(
        ((rest, rest_hbm), (w1, w1_hbm), (w2, w2_hbm), (w3, w3_hbm), (w4, w4_hbm)))]
    for copy in stores:
        copy.start()

    for copy in v_copies:
        copy.wait_recv()
    for side, x in ((0, -1), (1, cx)):
        vv[pl.ds(grid.tile(0, x, 0), cy), :] = vx[side]
    for side, y in ((0, -1), (1, cy)):
        vv[pl.ds(grid.row(1, 0, y), cx, stride=grid.py), :] = vy[side]

    def make_coef(x, _):
        if lax.axis_size("gz") > 2:
            zrow = jnp.where(halo.even, vz[1, x], vz[0, x])
        else:
            zrow = vz[0, x]
        for g in range(grid.groups):
            r0 = grid.tile(0, x, g)
            r1 = grid.tile(1, x, g)
            after, before = halo.z_near(vv[pl.ds(grid.tile(2, x, g), SUB), :], zrow, g)
            values = (
                0.05 - 0.5 * vv[pl.ds(r0 + grid.py, SUB), :],
                0.05 + 0.5 * vv[pl.ds(r0 - grid.py, SUB), :],
                0.05 - 0.5 * vv[pl.ds(r1 + 1, SUB), :],
                0.05 + 0.5 * vv[pl.ds(r1 - 1, SUB), :],
                0.05 - 0.5 * after,
                0.05 + 0.5 * before,
            )
            for i, value in enumerate(values):
                coef[i, x, g] = value
        return 0

    lax.fori_loop(0, cx, make_coef, 0)

    flow2 = flow_ref.reshape(nf * cells, LANES)
    sends = []

    def block(c, e):
        b = jnp.maximum(list_ref[0, min(e, listed - 1)], 0)
        return flow2[pl.ds(c * SUB * cells + b, SUB, stride=cells), :]

    def dispatch(c):
        for k in range(team.size):
            dst = sd if k else rv
            for p in range(sd.shape[2]):
                pair = [block(c, (2 * p + h) * team.size + k) for h in range(2)]
                dst[c, k, p] = jnp.concatenate(pair, axis=0).astype(jnp.bfloat16)
        for k in range(1, team.size):
            sends.append(remote(sd.at[c, k], rv.at[c, k], team_send.at[c, k],
                                team_recv.at[c, k], members[k]))
            sends[-1].start()

    for stage in range(3):
        weight = (1.0 / 3.0, 0.5, 1.0)[stage]
        u = us[stage]
        for c in range(chunks):
            slot = stage * chunks + c
            first = c * SUB
            halo.receive(slot, u, first)

            def body(x, _):
                zrow = halo.z_row(slot, x)
                face = jnp.zeros((SUB, LANES), jnp.float32)
                for g in range(grid.groups):
                    ks = [coef[i, x, g] for i in range(6)]
                    for f in range(SUB):
                        k = f * grid.groups + g
                        row = grid.tile(first + f, x, g)
                        t = u[pl.ds(row, SUB), :]
                        za, zb = halo.z_near(t, zrow, k)
                        s = (ks[0] * u[pl.ds(row + grid.py, SUB), :]
                             + ks[1] * u[pl.ds(row - grid.py, SUB), :])
                        s = s + (ks[2] * u[pl.ds(row + 1, SUB), :]
                                 + ks[3] * u[pl.ds(row - 1, SUB), :])
                        s = s + (ks[4] * za + ks[5] * zb)
                        q = t if stage == 0 else us[0][pl.ds(row, SUB), :]
                        r = q + weight * (s - 0.3 * t)
                        if stage == 2:
                            flow_ref[first + f, x, pl.ds(g * SUB, SUB)] = r
                        else:
                            us[stage + 1][pl.ds(row, SUB), :] = r
                            face = halo.pack_z(face, r, k)
                if stage < 2:
                    zs[slot + chunks, x] = face
                return 0

            lax.fori_loop(0, cx, body, 0)
            if stage < 2:
                halo.send(slot + chunks, us[stage + 1], first)
            else:
                dispatch(c)
                part = pl.ds(first, SUB)
                stores.append(pltpu.make_async_copy(
                    flow_ref.at[part], out_hbm.at[part], out_sem.at[c]))
                stores[-1].start()
    for copy in counts + sends:
        copy.wait_recv()
    backs = [pltpu.make_async_copy(cr, count_hbm, back_sem.at[0]),
             pltpu.make_async_copy(rv, slot_hbm, back_sem.at[1])]
    for copy in backs:
        copy.start()
    for copy in v_copies + counts + sends:
        copy.wait_send()
    for slot in range(3 * chunks):
        halo.finish(slot)
    for copy in stores + backs:
        copy.wait()


def layer(w, src, dst, step):
    rows = dst.shape[0] - 16
    for m in range(0, rows, step):
        k = min(step, rows - m)
        h = jnp.dot(w[m:m + k], src, preferred_element_type=jnp.float32)
        dst[m:m + k] = (h + h * jnp.tanh(h)).astype(jnp.bfloat16)


def network(x, w1, w2, w3, w4, h1, h2, h3):
    layer(w1, x, h1, 400)
    layer(w2, h1[...], h2, 400)
    layer(w3, h2[...], h3, 400)
    return jnp.dot(w4[...], h3[...], preferred_element_type=jnp.float32)


def bias_ones(rows, lanes):
    return jnp.where(lax.broadcasted_iota(jnp.int32, (rows, lanes), 0) < 3, 1.0, 0.0)


def chem_kernel(nf, cells, group, size, list_ref, count_ref, slots, rest, w1, w2, w3,
                w4, ret_ref, where_ref, todo, x_in, h1, h2, h3, inc, res):
    listed = list_ref.shape[0]
    n_lanes = group * LANES
    chunks = nf // SUB
    halves = slots.shape[1]
    cap = 2 * halves // size
    x_in[nf:nf + SUB] = bias_ones(SUB, n_lanes)
    for h in (h1, h2, h3):
        h[h.shape[0] - 16:] = bias_ones(16, n_lanes).astype(jnp.bfloat16)
    res[...] = jnp.zeros_like(res)

    def clear(i, _):
        for j in range(SUB):
            where_ref[i * SUB + j] = size * cap
        return 0

    lax.fori_loop(0, cells // SUB, clear, 0)

    def note(i, _):
        for j in range(SUB):
            e = i * SUB + j
            entry = list_ref[e]
            where_ref[jnp.where(entry >= 0, entry, cells)] = (
                lax.rem(e, size) * cap + e // size)
        return 0

    lax.fori_loop(0, listed // SUB, note, 0)

    def pick(k, n):
        have = count_ref[k, 0, 0]
        for s in range(cap):
            todo[n] = k * cap + s
            n = n + jnp.where(s * size + k < have, 1, 0)
        return n

    count = lax.fori_loop(0, size, pick, 0)

    def run(g, _):
        base = g * group
        for i in range(group):
            slot = jnp.where(base + i < count, todo[base + i], 0)
            for c in range(chunks):
                tile = slots[c, slot // 2].astype(jnp.float32)
                x_in[c * SUB:(c + 1) * SUB, i * LANES:(i + 1) * LANES] = jnp.where(
                    lax.rem(slot, 2) == 0, tile[:SUB], tile[SUB:])
        inc[...] = network(x_in[...].astype(jnp.bfloat16), w1, w2, w3, w4, h1, h2, h3)
        for i in range(group):
            slot = jnp.where(base + i < count, todo[base + i], size * cap)
            for c in range(chunks):
                res[c, slot] = inc[c * SUB:(c + 1) * SUB, i * LANES:(i + 1) * LANES] - rest[
                    c * SUB:(c + 1) * SUB]
        return 0

    lax.fori_loop(0, (count + group - 1) // group, run, 0)
    for c in range(chunks):
        for p in range(halves):
            pair = jnp.concatenate([res[c, 2 * p], res[c, 2 * p + 1]], axis=0)
            ret_ref[c, p] = pair.astype(jnp.bfloat16)


def diffuse_kernel(nf, cx, cy, d_ref, where_ref, owner_ref, q_hbm, ret_hbm, rest_ref, out_hbm, act_out,
                   u_ref, new_ref, ret, got_ret, res, part, got, act_send, act_recv,
                   xs, xr, ys, yr, zs, zr, send_sem, recv_sem,
                   team_send, team_recv, in_sem, out_sem, ret_sem):
    grid = Grid(cx, cy)
    chunks = nf // SUB
    team = Team()
    pairs = ret.shape[2]
    cap = 2 * pairs
    own = pltpu.make_async_copy(ret_hbm, ret, ret_sem)
    own.start()
    loads = []
    for c in range(chunks):
        loads.append(pltpu.make_async_copy(
            q_hbm.at[pl.ds(c * SUB, SUB)],
            u_ref.at[pl.ds(c * SUB, SUB), pl.ds(1, cx), pl.ds(SUB, cy)], in_sem.at[c]))
        loads[-1].start()
    near = neighbours()
    groups = [peers(a) for a in AXES[::-1]]
    members = [team.member(team.size - k) for k in range(team.size)]
    enter([to for g in groups for to in g] + members[1:])
    halo = Halo(grid, SUB, near, xs, xr, ys, yr, zs, zr, send_sem, recv_sem)
    lane = lane_ids()
    u2 = u_ref.reshape(nf * grid.px * grid.py, LANES)
    own.wait()
    backs = [[remote(ret.at[c, k], got_ret.at[c, k], team_send.at[c, k], team_recv.at[c, k],
                     members[k]) for k in range(1, team.size)] for c in range(chunks)]
    for copies in backs:
        for copy in copies:
            copy.start()

    def hops(phase):
        return [remote(part.at[phase], got.at[phase, k], act_send.at[phase, k],
                       act_recv.at[phase, k], to)
                for k, to in enumerate(groups[phase])]

    def gather(phase):
        for h in hops(phase):
            h.wait_recv()
        total = part[phase]
        for k in range(len(groups[phase])):
            total = total + got[phase, k]
        return total

    flat = lax.broadcasted_iota(jnp.int32, (SUB, LANES), 0) * LANES + lane

    def heat():
        total = jnp.zeros((SUB, LANES), jnp.float32)
        for e in range(owner_ref.shape[0]):
            r = res[0, (e % team.size) * cap + e // team.size][0:1]
            warm = jnp.sum(r * r, axis=1, keepdims=True) * (1.0 / (8.0 * LANES))
            total = total + jnp.where(flat == owner_ref[e], warm, 0.0)
        return total

    for c in range(chunks):
        loads[c].wait()
        res[c, team.size * cap] = jnp.zeros((SUB, LANES), jnp.float32)
        rest = rest_ref[c * SUB:(c + 1) * SUB]
        for copy in backs[c]:
            copy.wait_recv()
        for k in range(team.size):
            for p in range(pairs):
                tile = (got_ret if k else ret)[c, k, p].astype(jnp.float32)
                res[c, k * cap + 2 * p] = tile[:SUB] + rest
                res[c, k * cap + 2 * p + 1] = tile[SUB:] + rest

        def add(x, _):
            for y in range(cy):
                t = res[c, where_ref[x * cy + y]]
                at = pl.ds(grid.row(c * SUB, x, y), SUB, stride=grid.px * grid.py)
                u2[at, :] = u2[at, :] + t
            return 0

        lax.fori_loop(0, cx, add, 0)
        halo.load_z(c, u2, c * SUB)
        halo.send(c, u2, c * SUB)
        if c == 0:
            part[0] = heat()
            for h in hops(0):
                h.start()
    stores = []
    for c in range(chunks):
        if c < len(groups) - 1:
            part[c + 1] = gather(c)
            for h in hops(c + 1):
                h.start()
        first = c * SUB
        halo.receive(c, u2, first)

        def body(x, _):
            zrow = halo.z_row(c, x)
            for f in range(SUB):
                rate = d_ref[first + f]
                for g in range(grid.groups):
                    row = grid.tile(first + f, x, g)
                    t = u2[pl.ds(row, SUB), :]
                    za, zb = halo.z_near(t, zrow, f * grid.groups + g)
                    s = u2[pl.ds(row + grid.py, SUB), :] + u2[pl.ds(row - grid.py, SUB), :]
                    s = s + (u2[pl.ds(row + 1, SUB), :] + u2[pl.ds(row - 1, SUB), :])
                    s = s + (za + zb)
                    new_ref[first + f, x, pl.ds(g * SUB, SUB)] = t + rate * (s - 6.0 * t)
            return 0

        lax.fori_loop(0, cx, body, 0)
        chunk = pl.ds(first, SUB)
        stores.append(pltpu.make_async_copy(new_ref.at[chunk], out_hbm.at[chunk], out_sem.at[c]))
        stores[-1].start()
    done = min(chunks, len(groups) - 1)
    for phase in range(done, len(groups) - 1):
        part[phase + 1] = gather(phase)
        for h in hops(phase + 1):
            h.start()
    total = gather(len(groups) - 1)
    me = (lax.axis_index("gx") * lax.axis_size("gy") + lax.axis_index("gy")) * lax.axis_size(
        "gz") + lax.axis_index("gz")
    act_out[0] = jnp.sum(jnp.where(flat == me, total, 0.0))
    for phase in range(len(groups)):
        for h in hops(phase):
            h.wait_send()
    for copies in backs:
        for copy in copies:
            copy.wait_send()
    for c in range(chunks):
        halo.finish(c)
    for copy in stores:
        copy.wait()


def halo_scratch(slots, cx, cy):
    return [
        pltpu.VMEM((slots, 2, SUB, cy, LANES), jnp.bfloat16),
        pltpu.VMEM((slots, 2, SUB, cy, LANES), jnp.bfloat16),
        pltpu.VMEM((slots, 2, SUB, cx, LANES), jnp.float32),
        pltpu.VMEM((slots, 2, SUB, cx, LANES), jnp.float32),
        pltpu.VMEM((slots, cx, SUB, LANES), jnp.float32),
        pltpu.VMEM((slots, 2, cx, SUB, LANES), jnp.float32),
        pltpu.SemaphoreType.DMA((slots, 6)),
        pltpu.SemaphoreType.DMA((slots, 6)),
    ]


def spec(space, n=1):
    return [pl.BlockSpec(memory_space=space)] * n


def local(fields, velocity, diffusivity, weight_in, bias_in, weight_mid, bias_mid,
          weight_low, bias_low, weight_out, bias_out, react_list, owner_table):
    nf, cx, cy, cz = fields.shape
    chunks = nf // SUB
    cells = cx * cy
    padded = (cx + 2, cy + 2 * SUB, cz)
    slots = 3 * chunks
    dma = pltpu.SemaphoreType.DMA
    f32, bf16 = jnp.float32, jnp.bfloat16
    listed = react_list.shape[1]
    team = Team()
    size, cap = team.size, team.slots(listed)
    traffic = (chunks, size, cap // 2, 2 * SUB, LANES)
    h = (weight_in.shape[1], weight_mid.shape[1], weight_low.shape[1])
    wide = up(h[0], LANES)
    bias_wide = up(h[1], LANES) + up(h[2], LANES) + up(nf, LANES)
    w_shapes = [(wide, 32), (h[1], h[0] + 16), (h[2], h[1] + 16), (nf, h[2] + 16)]

    flowed, sent, counts, rest, w1, w2, w3, w4 = pl.pallas_call(
        functools.partial(flow_kernel, nf, cx, cy),
        out_shape=(jax.ShapeDtypeStruct(fields.shape, f32),
                   jax.ShapeDtypeStruct(traffic, bf16),
                   jax.ShapeDtypeStruct((size, 1, LANES), jnp.int32),
                   jax.ShapeDtypeStruct((nf, LANES), f32))
        + tuple(jax.ShapeDtypeStruct(w, bf16) for w in w_shapes),
        in_specs=spec(pltpu.HBM, 11),
        out_specs=tuple(spec(pl.ANY, 8)),
        scratch_shapes=[pltpu.SMEM((1, listed), jnp.int32)]
        + [pltpu.VMEM((nf,) + padded, f32)] * 3 + [
            pltpu.VMEM((3,) + padded, f32),
            pltpu.VMEM((nf, cx, cy, cz), f32),
            pltpu.VMEM((6, cx, cy // SUB, SUB, cz), f32),
            pltpu.VMEM(traffic, bf16),
            pltpu.VMEM(traffic, bf16),
            pltpu.VMEM((1, LANES), jnp.int32),
            pltpu.VMEM((size, 1, LANES), jnp.int32),
            pltpu.VMEM((nf, h[0]), bf16),
            pltpu.VMEM((h[1], h[0]), bf16),
            pltpu.VMEM((h[2], h[1]), bf16),
            pltpu.VMEM((nf, h[2]), bf16),
            pltpu.VMEM((h[0],), f32),
            pltpu.VMEM((h[1],), f32),
            pltpu.VMEM((h[2],), f32),
            pltpu.VMEM((nf,), f32),
            pltpu.VMEM((32, wide), f32),
            pltpu.VMEM((32, bias_wide), f32),
            pltpu.VMEM((bias_wide, 32), bf16),
        ] + [pltpu.VMEM(w, bf16) for w in w_shapes] + [
            pltpu.VMEM((h[0] + 16, LANES), bf16),
            pltpu.VMEM((h[1] + 16, LANES), bf16),
            pltpu.VMEM((h[2] + 16, LANES), bf16),
            pltpu.VMEM((nf, LANES), f32),
            pltpu.VMEM((2, cy, cz), f32),
            pltpu.VMEM((2, cx, cz), f32),
            pltpu.VMEM((2, cx, SUB, cz), f32),
            pltpu.VMEM((2, cx, cz), f32),
            pltpu.VMEM((cx, SUB, cz), f32),
        ] + halo_scratch(slots, cx, cy) + [
            dma((6,)), dma((6,)), dma((chunks + 1,)), dma((chunks,)),
            dma((chunks + 1, size)), dma((chunks + 1, size)), dma((9,)), dma((5,)), dma((2,))],
        compiler_params=pltpu.CompilerParams(
            collective_id=0, has_side_effects=True, vmem_limit_bytes=48 * MIB),
        name="flow",
    )(*[pltpu.with_memory_space_constraint(a, pltpu.HBM) for a in (
        react_list, fields, velocity, weight_in, weight_mid.T, weight_low.T, weight_out.T,
        bias_in, bias_mid, bias_low, bias_out)])

    group = 4
    n_lanes = group * LANES
    halves = size * cap // 2
    ret, where = pl.pallas_call(
        functools.partial(chem_kernel, nf, cells, group, size),
        out_shape=(jax.ShapeDtypeStruct((chunks, halves, 2 * SUB, LANES), bf16),
                   jax.ShapeDtypeStruct((cells + SUB,), jnp.int32)),
        in_specs=spec(pltpu.SMEM, 2) + spec(pltpu.VMEM, 6),
        out_specs=(spec(pltpu.VMEM)[0], spec(pltpu.SMEM)[0]),
        scratch_shapes=[
            pltpu.SMEM((size * cap + group,), jnp.int32),
            pltpu.VMEM((nf + SUB, n_lanes), f32),
            pltpu.VMEM((h[0] + 16, n_lanes), bf16),
            pltpu.VMEM((h[1] + 16, n_lanes), bf16),
            pltpu.VMEM((h[2] + 16, n_lanes), bf16),
            pltpu.VMEM((nf, n_lanes), f32),
            pltpu.VMEM((chunks, size * cap + 1, SUB, LANES), f32),
        ],
        compiler_params=pltpu.CompilerParams(vmem_limit_bytes=40 * MIB),
        name="chem",
    )(react_list[0], counts, sent.reshape(chunks, halves, 2 * SUB, LANES), rest,
      w1, w2, w3, w4)

    most = max(lax.axis_size(a) for a in AXES) - 1
    updated, mine = pl.pallas_call(
        functools.partial(diffuse_kernel, nf, cx, cy),
        out_shape=(jax.ShapeDtypeStruct(fields.shape, f32),
                   jax.ShapeDtypeStruct((1,), f32)),
        in_specs=spec(pltpu.SMEM, 3) + spec(pl.ANY, 2) + spec(pltpu.VMEM),
        out_specs=(spec(pl.ANY)[0], spec(pltpu.SMEM)[0]),
        scratch_shapes=[
            pltpu.VMEM((nf,) + padded, f32),
            pltpu.VMEM((nf, cx, cy, cz), f32),
            pltpu.VMEM(traffic, bf16),
            pltpu.VMEM(traffic, bf16),
            pltpu.VMEM((chunks, size * cap + 1, SUB, LANES), f32),
            pltpu.VMEM((len(AXES), SUB, LANES), f32),
            pltpu.VMEM((len(AXES), most, SUB, LANES), f32),
            dma((len(AXES), most)),
            dma((len(AXES), most)),
        ] + halo_scratch(chunks, cx, cy) + [
            dma((chunks, size)), dma((chunks, size)), dma((chunks,)), dma((chunks,)), dma],
        compiler_params=pltpu.CompilerParams(
            collective_id=1, has_side_effects=True, vmem_limit_bytes=48 * MIB),
        name="diffuse",
    )(diffusivity, where, owner_table[0], flowed, ret.reshape(traffic), rest)
    return updated, mine


def solution(mesh):
    return jax.shard_map(
        local,
        mesh=mesh,
        in_specs=(P(None, *AXES), P(None, *AXES)) + (P(),) * 9
        + (P(AXES, None), P(AXES, None)),
        out_specs=(P(None, *AXES), P(AXES)),
        check_vma=False,
    )
```

time: 160 us -> 111 us (0.69)
  Pallas kernels: 147 us -> 106 us
  local copies, waits for them, and re-layouts: 5.56 us -> 1.68 us
  other arithmetic: 3.65 us -> 0 us
    pallas_call x1, Pallas kernels: 78.1 us -> 25.2 us  [local(): pl.pallas_call(functools.partial(diffuse_kernel, nf, cx, cy), out_shape=(...]
    pallas_call x2, Pallas kernels: 69 us -> 80.6 us  [the longest x1 51.3 us: local(): pl.pallas_call(functools.partial(flow_kernel, nf, cx, cy), out_shape=(jax...]
    unnamed x17 -> x7, local copies, waits for them, and re-layouts: 4.58 us -> 1.68 us
    mul x3 -> x0, other arithmetic: 2.27 us -> none  [the longest x1 0.9 us: local(): weight_in.T * half]
where the time goes in v2:
time: 111 us; the launch traced here: 110 us
  Pallas kernels  106 us (95%)
  between operations  2.51 us (2%)
  local copies, waits for them, and re-layouts  1.68 us (2%)
    pallas_call x1, Pallas kernels, local(): pl.pallas_call(functools.partial(flow_kernel, nf, cx, cy), out_shape=(jax...  51.3 us
    pallas_call x1, Pallas kernels, local(): pl.pallas_call(functools.partial(chem_kernel, nf, cells, group, size), ou...  29.4 us
    pallas_call x1, Pallas kernels, local(): pl.pallas_call(functools.partial(diffuse_kernel, nf, cx, cy), out_shape=(...  25.2 us

profile of v2, /device:TPU:0, one launch (start us, length us, event | category | flops | bytes accessed | tf_op | source)
XLA Modules:
  0.0 110.0 jit_solution(17497375709322444856)
XLA Ops:
  0.6 0.0 copy-start
  0.6 51.3 %flow.1 = (f32[24,8,32,128]{3,2,1,0:T(8,128)}, bf16[3,16,3,16,128]{4,3,2,1,0:T(8,128)(2,1)S(1)}, s32[16,1,128]{2,1,0:T(1,128)S(1)}, f32[24,128]{1,0:T(8,128)S(1)...) custom-call(s32[1,96]{1,0:T(1,128)} %list_hbm.1, ...), custom_call_target="tpu_custom_call" | custom-call | tf_op jit(solution)/shard_map/flow/pallas_call | solution.py:656
  51.9 0.0 copy-start.1
  51.9 0.0 copy-start.2
  51.9 0.0 copy-done
  52.0 29.4 %chem.1 = (bf16[3,48,16,128]{3,2,1,0:T(8,128)(2,1)S(1)}, s32[264]{0:T(512)S(1)}) custom-call(s32[96]{0:T(128)S(1)} %bitcast.9, s32[16,1,128]{2,1,0:T(1,128)S(1)} %get-tuple-element.12.count_ref, bf16[3,48,16,128]{3,2,1,0:T(8,128)(2,1)S(1)} %bitcast.7, f32[24,128]{1,0:T(8,128)S(1)} %get-tuple-element.14.rest.rest_ref, ...), custom_call_target="tpu_custom_call" | custom-call | tf_op jit(solution)/shard_map/chem/pallas_call | solution.py:708
  81.3 0.0 copy-done.1
  81.4 0.0 copy-done.2
  81.4 25.2 %diffuse.1 = (f32[24,8,32,128]{3,2,1,0:T(8,128)S(1)}, f32[1]{0:T(128)}) custom-call(f32[24]{0:T(128)S(1)} %copy-done.1, s32[264]{0:T(512)S(1)} %get-tuple-element.19.where_ref, s32[96]{0:T(128)S(1)} %bitcast.10, f32[24,8,32,128]{3,2,1,0:T(8,128)} %get-tuple-element.20.q_hbm, bf16[3,16,3,16,128]{4,3,2,1,0:T(8,128)(2,1)S(1)} %bitcast.8, ...), custom_call_target="tpu_custom_call" | custom-call | tf_op jit(solution)/shard_map/diffuse/pallas_call | solution.py:729
  106.6 1.7 %copy.17 = f32[24,8,32,128]{3,2,1,0:T(8,128)} copy(f32[24,8,32,128]{3,2,1,0:T(8,128)S(1)} %get-tuple-element.24) | data formatting | bytes 6291456
Async XLA Ops:
  0.6 51.3 %copy-start = (s32[1,96]{1,0:T(1,128)S(1)}, s32[1,96]{1,0:T(1,128)}, u32[]{:S(2)}) copy-start(s32[1,96]{1,0:T(1,128)} %list_hbm.1) | copy-start | bytes 1156
  51.9 29.4 %copy-start.1 = (f32[24]{0:T(128)S(1)}, f32[24]{0:T(128)}, u32[]{:S(2)}) copy-start(f32[24]{0:T(128)} %d_ref.1) | copy-start | bytes 292
  51.9 29.4 %copy-start.2 = (s32[1,96]{1,0:T(1,128)S(1)}, s32[1,96]{1,0:T(1,128)}, u32[]{:S(2)}) copy-start(s32[1,96]{1,0:T(1,128)} %param.25) | copy-start | bytes 1156

commit v3 on v2

--- a/solution.py
+++ b/solution.py
@@ -27,11 +27,14 @@
     return out
 
 
-def enter(targets):
+def greet(targets):
     barrier = pltpu.get_barrier_semaphore()
     for to in targets:
         pl.semaphore_signal(barrier, inc=1, device_id=to, device_id_type=MESH)
-    pl.semaphore_wait(barrier, len(targets))
+
+
+def met(targets):
+    pl.semaphore_wait(pltpu.get_barrier_semaphore(), len(targets))
 
 
 def peers(axis):
@@ -55,10 +58,18 @@
     return lax.broadcasted_iota(jnp.int32, (SUB, LANES), 1)
 
 
+def odd_tiles(n):
+    return n if n // SUB % 2 else n + SUB
+
+
+def padded(cx, cy):
+    return cx + 2 + (cx + 1) % 2, odd_tiles(cy + 2 * SUB), LANES
+
+
 class Grid:
     def __init__(self, cx, cy):
         self.cx, self.cy = cx, cy
-        self.px, self.py = cx + 2, cy + 2 * SUB
+        self.px, self.py, _ = padded(cx, cy)
         self.groups = cy // SUB
 
     def row(self, f, x, y=0):
@@ -79,7 +90,7 @@
         self.even = lax.rem(lane, 2) == 0
         self.pair = lax.rem(lane + 1, LANES) // 2
 
-    def copies(self, slot):
+    def copies(self, slot, first=0, last=6):
         (xu, xd), (yu, yd), (zu, zd) = self.near
         plan = [
             (self.xs.at[slot, 1], self.xr.at[slot, 0], xu),
@@ -92,7 +103,7 @@
             plan.append((self.zs.at[slot], self.zr.at[slot, 1], zd))
         return [
             remote(s, d, self.send_sem.at[slot, i], self.recv_sem.at[slot, i], to)
-            for i, (s, d, to) in enumerate(plan)
+            for i, (s, d, to) in enumerate(plan) if first <= i < last
         ]
 
     def pack_z(self, face, t, k):
@@ -109,28 +120,37 @@
         before = pltpu.roll(jnp.where(self.last, r, t), 1, 1)
         return after, before
 
-    def send(self, slot, u, base):
+    def pack_x(self, slot, u, base):
         grid = self.grid
         for f in range(self.width):
             for side, x in ((0, 0), (1, grid.cx - 1)):
                 self.xs[slot, side, f] = u[
                     pl.ds(grid.tile(base + f, x, 0), grid.cy), :].astype(jnp.bfloat16)
+
+    def send_x(self, slot):
+        for c in self.copies(slot, 0, 2):
+            c.start()
+
+    def send_yz(self, slot, u, base):
+        grid = self.grid
+        for f in range(self.width):
             for side, y in ((0, 0), (1, grid.cy - 1)):
                 self.ys[slot, side, f] = u[
                     pl.ds(grid.row(base + f, 0, y), grid.cx, stride=grid.py), :]
-        for c in self.copies(slot):
+        for c in self.copies(slot, 2):
             c.start()
 
     def load_z(self, slot, u, base):
         grid = self.grid
 
-        def body(x, _):
-            face = jnp.zeros((SUB, LANES), jnp.float32)
-            for g in range(grid.groups):
-                for f in range(self.width):
-                    t = u[pl.ds(grid.tile(base + f, x, g), SUB), :]
-                    face = self.pack_z(face, t, f * grid.groups + g)
-            self.zs[slot, x] = face
+        def body(i, _):
+            for x in [i]:
+                face = jnp.zeros((SUB, LANES), jnp.float32)
+                for g in range(grid.groups):
+                    for f in range(self.width):
+                        t = u[pl.ds(grid.tile(base + f, x, g), SUB), :]
+                        face = self.pack_z(face, t, f * grid.groups + g)
+                self.zs[slot, x] = face
             return 0
 
         lax.fori_loop(0, grid.cx, body, 0)
@@ -207,31 +227,31 @@
 
 def flow_kernel(nf, cx, cy, list_hbm, q_hbm, v_hbm, wi_hbm, wm_hbm, wl_hbm, wo_hbm,
                 b1_hbm, b2_hbm, b3_hbm, b4_hbm,
-                out_hbm, slot_hbm, count_hbm, rest_hbm, w1_hbm, w2_hbm, w3_hbm, w4_hbm,
-                list_ref, u0, u1, u2, w_ref, flow_ref, coef, sd, rv, cs, cr,
-                wi, wm, wl, wo, b1, b2, b3, b4, t1, t2, cols, w1, w2, w3, w4,
-                h1, h2, h3, rest,
+                out_hbm, rv, cr, where_ref, rest, w1, w2, w3, w4,
+                list_ref, u0, u1, u2, w_ref, flow_ref, coef, sd, cs,
+                wi, wm, wl, wo, b1, b2, b3, b4, t1, t2, cols, h1, h2, h3,
                 vx, vy, vz, vys, vzs, xs, xr, ys, yr, zs, zr,
                 send_sem, recv_sem, vs_sem, vr_sem, in_sem, out_sem,
-                team_send, team_recv, w_in, w_out, back_sem):
+                team_send, team_recv, w_in, tally_ref, tally_sem):
     grid = Grid(cx, cy)
     chunks = nf // SUB
     cells = cx * cy
     team = Team()
     listed = list_ref.shape[1]
-    loads = [pltpu.make_async_copy(
-        v_hbm, w_ref.at[:, pl.ds(1, cx), pl.ds(SUB, cy)], in_sem.at[chunks])]
-    for c in range(chunks):
-        loads.append(pltpu.make_async_copy(
-            q_hbm.at[pl.ds(c * SUB, SUB)],
-            u0.at[pl.ds(c * SUB, SUB), pl.ds(1, cx), pl.ds(SUB, cy)], in_sem.at[c]))
-    for i, (src, dst) in enumerate((
-            (wi_hbm, wi), (b1_hbm, b1), (b2_hbm, b2), (b3_hbm, b3), (b4_hbm, b4),
-            (wo_hbm, wo), (list_hbm, list_ref), (wl_hbm, wl), (wm_hbm, wm))):
-        loads.append(pltpu.make_async_copy(src, dst, w_in.at[i]))
-    for copy in loads:
+    def fetch(c, kind, x, n):
+        return pltpu.make_async_copy(
+            q_hbm.at[pl.ds(c * SUB, SUB), pl.ds(x, n)],
+            u0.at[pl.ds(c * SUB, SUB), pl.ds(1 + x, n), pl.ds(SUB, cy)], in_sem.at[c, kind])
+
+    faces = [[fetch(c, 0, 0, 1), fetch(c, 1, cx - 1, 1)] for c in range(chunks)]
+    inner = [fetch(c, 2, 1, cx - 2) for c in range(chunks)]
+    v_load = pltpu.make_async_copy(
+        v_hbm, w_ref.at[:, pl.ds(1, cx), pl.ds(SUB, cy)], in_sem.at[0, 3])
+    w_loads = [pltpu.make_async_copy(src, dst, w_in.at[i]) for i, (src, dst) in enumerate((
+        (wi_hbm, wi), (b1_hbm, b1), (b2_hbm, b2), (b3_hbm, b3), (b4_hbm, b4),
+        (wo_hbm, wo), (list_hbm, list_ref), (wl_hbm, wl), (wm_hbm, wm)))]
+    for copy in sum(faces, []) + [v_load] + inner:
         copy.start()
-    w_loads = loads[1 + chunks:]
     near = neighbours()
     (xu, xd), (yu, yd), (zu, zd) = near
     halo = Halo(grid, SUB, near, xs, xr, ys, yr, zs, zr, send_sem, recv_sem)
@@ -239,9 +259,16 @@
     us = [u.reshape(rows, LANES) for u in (u0, u1, u2)]
     vv = w_ref.reshape(3 * grid.px * grid.py, LANES)
     members = [team.member(k) for k in range(team.size)]
-    enter([to for pair in near for to in pair] + members[1:])
-
-    loads[0].wait()
+    known = [to for pair in near for to in pair] + members[1:]
+    greet(known)
+    for c in range(chunks):
+        for copy in faces[c]:
+            copy.wait()
+        halo.pack_x(c, us[0], c * SUB)
+        if c == 0:
+            met(known)
+        halo.send_x(c)
+    v_load.wait()
     for side, y in ((0, 0), (1, cy - 1)):
         vys[side] = vv[pl.ds(grid.row(1, 0, y), cx, stride=grid.py), :]
 
@@ -266,10 +293,13 @@
                 for i, (s, d, to) in enumerate(plan)]
     for copy in v_copies:
         copy.start()
+    for copy in inner:
+        copy.wait()
+    for copy in w_loads:
+        copy.start()
     for c in range(chunks):
-        loads[1 + c].wait()
         halo.load_z(c, us[0], c * SUB)
-        halo.send(c, us[0], c * SUB)
+        halo.send_yz(c, us[0], c * SUB)
 
     for copy in w_loads:
         copy.wait()
@@ -300,10 +330,6 @@
     origin = jnp.concatenate(
         [jnp.zeros((nf, LANES), jnp.float32), bias_ones(w1.shape[1] - nf, LANES)], axis=0)
     rest[...] = network(origin.astype(jnp.bfloat16), w1, w2, w3, w4, h1, h2, h3)
-    stores = [pltpu.make_async_copy(src, dst, w_out.at[i]) for i, (src, dst) in enumerate(
-        ((rest, rest_hbm), (w1, w1_hbm), (w2, w2_hbm), (w3, w3_hbm), (w4, w4_hbm)))]
-    for copy in stores:
-        copy.start()
 
     for copy in v_copies:
         copy.wait_recv()
@@ -335,18 +361,37 @@
 
     lax.fori_loop(0, cx, make_coef, 0)
 
-    flow2 = flow_ref.reshape(nf * cells, LANES)
-    sends = []
-
-    def block(c, e):
-        b = jnp.maximum(list_ref[0, min(e, listed - 1)], 0)
-        return flow2[pl.ds(c * SUB * cells + b, SUB, stride=cells), :]
+    room = flow_ref.shape[1]
+    cap = 2 * sd.shape[2]
+    for copy in counts:
+        copy.wait_recv()
+    tally = pltpu.make_async_copy(cr, tally_ref, tally_sem)
+    tally.start()
+    tally.wait()
+    me = team.place()
+    ahead = lax.fori_loop(1, team.size, lambda k, n: n + jnp.where(
+        k <= me, tally_ref[k, 0, 0], 0), 0)
+    shift = lax.rem(ahead + team.size - me, team.size)
+    home = lax.broadcasted_iota(jnp.int32, where_ref.shape, 0) * LANES + (
+        lax.broadcasted_iota(jnp.int32, where_ref.shape, 1))
+    table = jnp.where(home == cells, shift, team.size * cap)
+    for e in range(listed):
+        slot = lax.rem(shift + e, team.size) * cap + e // team.size
+        table = jnp.where(home == list_ref[0, e], slot, table)
+    where_ref[...] = table
+    flow2 = flow_ref.reshape(nf * room, LANES)
+    sends, stores = [], []
+
+    def block(c, s, k):
+        e = s * team.size + lax.rem(k + team.size - shift, team.size)
+        b = jnp.maximum(list_ref[0, jnp.minimum(e, listed - 1)], 0)
+        return flow2[pl.ds(c * SUB * room + b, SUB, stride=room), :]
 
     def dispatch(c):
         for k in range(team.size):
             dst = sd if k else rv
             for p in range(sd.shape[2]):
-                pair = [block(c, (2 * p + h) * team.size + k) for h in range(2)]
+                pair = [block(c, 2 * p + h, k) for h in range(2)]
                 dst[c, k, p] = jnp.concatenate(pair, axis=0).astype(jnp.bfloat16)
         for k in range(1, team.size):
             sends.append(remote(sd.at[c, k], rv.at[c, k], team_send.at[c, k],
@@ -361,52 +406,52 @@
             first = c * SUB
             halo.receive(slot, u, first)
 
-            def body(x, _):
-                zrow = halo.z_row(slot, x)
-                face = jnp.zeros((SUB, LANES), jnp.float32)
-                for g in range(grid.groups):
-                    ks = [coef[i, x, g] for i in range(6)]
-                    for f in range(SUB):
-                        k = f * grid.groups + g
-                        row = grid.tile(first + f, x, g)
-                        t = u[pl.ds(row, SUB), :]
-                        za, zb = halo.z_near(t, zrow, k)
-                        s = (ks[0] * u[pl.ds(row + grid.py, SUB), :]
-                             + ks[1] * u[pl.ds(row - grid.py, SUB), :])
-                        s = s + (ks[2] * u[pl.ds(row + 1, SUB), :]
-                                 + ks[3] * u[pl.ds(row - 1, SUB), :])
-                        s = s + (ks[4] * za + ks[5] * zb)
-                        q = t if stage == 0 else us[0][pl.ds(row, SUB), :]
-                        r = q + weight * (s - 0.3 * t)
-                        if stage == 2:
-                            flow_ref[first + f, x, pl.ds(g * SUB, SUB)] = r
-                        else:
-                            us[stage + 1][pl.ds(row, SUB), :] = r
-                            face = halo.pack_z(face, r, k)
-                if stage < 2:
-                    zs[slot + chunks, x] = face
+            def body(i, _):
+                for x in [i]:
+                    zrow = halo.z_row(slot, x)
+                    face = jnp.zeros((SUB, LANES), jnp.float32)
+                    for g in range(grid.groups):
+                        ks = [coef[j, x, g] for j in range(6)]
+                        for f in range(SUB):
+                            k = f * grid.groups + g
+                            row = grid.tile(first + f, x, g)
+                            t = u[pl.ds(row, SUB), :]
+                            za, zb = halo.z_near(t, zrow, k)
+                            s = (ks[0] * u[pl.ds(row + grid.py, SUB), :]
+                                 + ks[1] * u[pl.ds(row - grid.py, SUB), :])
+                            s = s + (ks[2] * u[pl.ds(row + 1, SUB), :]
+                                     + ks[3] * u[pl.ds(row - 1, SUB), :])
+                            s = s + (ks[4] * za + ks[5] * zb)
+                            q = t if stage == 0 else us[0][pl.ds(row, SUB), :]
+                            r = q + weight * (s - 0.3 * t)
+                            if stage == 2:
+                                at = pl.multiple_of(x * cy + g * SUB, SUB)
+                                flow_ref[first + f, pl.ds(at, SUB)] = r
+                            else:
+                                us[stage + 1][pl.ds(row, SUB), :] = r
+                                face = halo.pack_z(face, r, k)
+                    if stage < 2:
+                        zs[slot + chunks, x] = face
                 return 0
 
             lax.fori_loop(0, cx, body, 0)
             if stage < 2:
-                halo.send(slot + chunks, us[stage + 1], first)
+                halo.pack_x(slot + chunks, us[stage + 1], first)
+                halo.send_x(slot + chunks)
+                halo.send_yz(slot + chunks, us[stage + 1], first)
             else:
                 dispatch(c)
                 part = pl.ds(first, SUB)
                 stores.append(pltpu.make_async_copy(
-                    flow_ref.at[part], out_hbm.at[part], out_sem.at[c]))
+                    flow_ref.at[part, pl.ds(0, cells)], out_hbm.at[part], out_sem.at[c]))
                 stores[-1].start()
-    for copy in counts + sends:
+    for copy in sends:
         copy.wait_recv()
-    backs = [pltpu.make_async_copy(cr, count_hbm, back_sem.at[0]),
-             pltpu.make_async_copy(rv, slot_hbm, back_sem.at[1])]
-    for copy in backs:
-        copy.start()
     for copy in v_copies + counts + sends:
         copy.wait_send()
     for slot in range(3 * chunks):
         halo.finish(slot)
-    for copy in stores + backs:
+    for copy in stores:
         copy.wait()
 
 
@@ -429,9 +474,8 @@
     return jnp.where(lax.broadcasted_iota(jnp.int32, (rows, lanes), 0) < 3, 1.0, 0.0)
 
 
-def chem_kernel(nf, cells, group, size, list_ref, count_ref, slots, rest, w1, w2, w3,
-                w4, ret_ref, where_ref, todo, x_in, h1, h2, h3, inc, res):
-    listed = list_ref.shape[0]
+def chem_kernel(nf, group, size, count_ref, slots, rest, w1, w2, w3,
+                w4, ret_ref, todo, x_in, h1, h2, h3, inc, res):
     n_lanes = group * LANES
     chunks = nf // SUB
     halves = slots.shape[1]
@@ -441,31 +485,19 @@
         h[h.shape[0] - 16:] = bias_ones(16, n_lanes).astype(jnp.bfloat16)
     res[...] = jnp.zeros_like(res)
 
-    def clear(i, _):
-        for j in range(SUB):
-            where_ref[i * SUB + j] = size * cap
-        return 0
-
-    lax.fori_loop(0, cells // SUB, clear, 0)
-
-    def note(i, _):
-        for j in range(SUB):
-            e = i * SUB + j
-            entry = list_ref[e]
-            where_ref[jnp.where(entry >= 0, entry, cells)] = (
-                lax.rem(e, size) * cap + e // size)
-        return 0
-
-    lax.fori_loop(0, listed // SUB, note, 0)
-
-    def pick(k, n):
+    me = Team().place()
+
+    def pick(m, carry):
+        ahead, n = carry
+        k = lax.rem(me + size - m, size)
         have = count_ref[k, 0, 0]
+        first = lax.rem(k + 2 * size - lax.rem(ahead + size - m, size), size)
         for s in range(cap):
             todo[n] = k * cap + s
-            n = n + jnp.where(s * size + k < have, 1, 0)
-        return n
-
-    count = lax.fori_loop(0, size, pick, 0)
+            n = n + jnp.where(s * size + first < have, 1, 0)
+        return ahead + have, n
+
+    count = lax.fori_loop(0, size, pick, (0, 0))[1]
 
     def run(g, _):
         base = g * group
@@ -491,13 +523,14 @@
 
 
 def diffuse_kernel(nf, cx, cy, d_ref, where_ref, owner_ref, q_hbm, ret_hbm, rest_ref, out_hbm, act_out,
-                   u_ref, new_ref, ret, got_ret, res, part, got, act_send, act_recv,
+                   u_ref, old_ref, new_ref, ret, got_ret, res, part, got, act_send, act_recv,
                    xs, xr, ys, yr, zs, zr, send_sem, recv_sem,
                    team_send, team_recv, in_sem, out_sem, ret_sem):
     grid = Grid(cx, cy)
     chunks = nf // SUB
     team = Team()
     pairs = ret.shape[2]
+    cells = cx * cy
     cap = 2 * pairs
     own = pltpu.make_async_copy(ret_hbm, ret, ret_sem)
     own.start()
@@ -505,16 +538,20 @@
     for c in range(chunks):
         loads.append(pltpu.make_async_copy(
             q_hbm.at[pl.ds(c * SUB, SUB)],
-            u_ref.at[pl.ds(c * SUB, SUB), pl.ds(1, cx), pl.ds(SUB, cy)], in_sem.at[c]))
+            old_ref.at[pl.ds(c * SUB, SUB), pl.ds(0, cells)], in_sem.at[c]))
         loads[-1].start()
     near = neighbours()
     groups = [peers(a) for a in AXES[::-1]]
     members = [team.member(team.size - k) for k in range(team.size)]
-    enter([to for g in groups for to in g] + members[1:])
+    known = [to for g in groups for to in g] + members[1:]
+    greet(known)
     halo = Halo(grid, SUB, near, xs, xr, ys, yr, zs, zr, send_sem, recv_sem)
     lane = lane_ids()
     u2 = u_ref.reshape(nf * grid.px * grid.py, LANES)
+    room = old_ref.shape[1]
+    old2 = old_ref.reshape(nf * room, LANES)
     own.wait()
+    met(known)
     backs = [[remote(ret.at[c, k], got_ret.at[c, k], team_send.at[c, k], team_recv.at[c, k],
                      members[k]) for k in range(1, team.size)] for c in range(chunks)]
     for copies in backs:
@@ -536,12 +573,23 @@
 
     flat = lax.broadcasted_iota(jnp.int32, (SUB, LANES), 0) * LANES + lane
 
+    listed = owner_ref.shape[0]
+
     def heat():
         total = jnp.zeros((SUB, LANES), jnp.float32)
-        for e in range(owner_ref.shape[0]):
-            r = res[0, (e % team.size) * cap + e // team.size][0:1]
-            warm = jnp.sum(r * r, axis=1, keepdims=True) * (1.0 / (8.0 * LANES))
-            total = total + jnp.where(flat == owner_ref[e], warm, 0.0)
+        shift = where_ref[cells // LANES, cells % LANES]
+
+        def body(k, total):
+            first = lax.rem(k + team.size - shift, team.size)
+            for s in range(cap):
+                r = res[0, k * cap + s][0:1]
+                warm = jnp.sum(r * r, axis=1, keepdims=True) * (1.0 / (8.0 * LANES))
+                e = s * team.size + first
+                owner = jnp.where(e < listed, owner_ref[jnp.minimum(e, listed - 1)], -1)
+                total = total + jnp.where(flat == owner, warm, 0.0)
+            return total
+
+        total = lax.fori_loop(0, team.size, body, total)
         return total
 
     for c in range(chunks):
@@ -556,16 +604,23 @@
                 res[c, k * cap + 2 * p] = tile[:SUB] + rest
                 res[c, k * cap + 2 * p + 1] = tile[SUB:] + rest
 
-        def add(x, _):
-            for y in range(cy):
-                t = res[c, where_ref[x * cy + y]]
-                at = pl.ds(grid.row(c * SUB, x, y), SUB, stride=grid.px * grid.py)
-                u2[at, :] = u2[at, :] + t
+        def add(i, _):
+            for x in [i]:
+                line, lane0 = x * cy // LANES, lax.rem(x * cy, LANES)
+                for y in range(cy):
+                    b = x * cy + y
+                    if LANES % cy:
+                        line, lane0 = b // LANES, lax.rem(b, LANES) - y
+                    t = res[c, where_ref[line, lane0 + y]]
+                    old = old2[pl.ds(c * SUB * room + b, SUB, stride=room), :]
+                    u2[pl.ds(grid.row(c * SUB, x, y), SUB, stride=grid.px * grid.py), :] = old + t
             return 0
 
         lax.fori_loop(0, cx, add, 0)
+        halo.pack_x(c, u2, c * SUB)
+        halo.send_x(c)
         halo.load_z(c, u2, c * SUB)
-        halo.send(c, u2, c * SUB)
+        halo.send_yz(c, u2, c * SUB)
         if c == 0:
             part[0] = heat()
             for h in hops(0):
@@ -579,18 +634,19 @@
         first = c * SUB
         halo.receive(c, u2, first)
 
-        def body(x, _):
-            zrow = halo.z_row(c, x)
-            for f in range(SUB):
-                rate = d_ref[first + f]
-                for g in range(grid.groups):
-                    row = grid.tile(first + f, x, g)
-                    t = u2[pl.ds(row, SUB), :]
-                    za, zb = halo.z_near(t, zrow, f * grid.groups + g)
-                    s = u2[pl.ds(row + grid.py, SUB), :] + u2[pl.ds(row - grid.py, SUB), :]
-                    s = s + (u2[pl.ds(row + 1, SUB), :] + u2[pl.ds(row - 1, SUB), :])
-                    s = s + (za + zb)
-                    new_ref[first + f, x, pl.ds(g * SUB, SUB)] = t + rate * (s - 6.0 * t)
+        def body(i, _):
+            for x in [i]:
+                zrow = halo.z_row(c, x)
+                for f in range(SUB):
+                    rate = d_ref[first + f]
+                    for g in range(grid.groups):
+                        row = grid.tile(first + f, x, g)
+                        t = u2[pl.ds(row, SUB), :]
+                        za, zb = halo.z_near(t, zrow, f * grid.groups + g)
+                        s = u2[pl.ds(row + grid.py, SUB), :] + u2[pl.ds(row - grid.py, SUB), :]
+                        s = s + (u2[pl.ds(row + 1, SUB), :] + u2[pl.ds(row - 1, SUB), :])
+                        s = s + (za + zb)
+                        new_ref[first + f, x, pl.ds(g * SUB, SUB)] = t + rate * (s - 6.0 * t)
             return 0
 
         lax.fori_loop(0, cx, body, 0)
@@ -640,7 +696,8 @@
     nf, cx, cy, cz = fields.shape
     chunks = nf // SUB
     cells = cx * cy
-    padded = (cx + 2, cy + 2 * SUB, cz)
+    box = padded(cx, cy)
+    room = odd_tiles(cells)
     slots = 3 * chunks
     dma = pltpu.SemaphoreType.DMA
     f32, bf16 = jnp.float32, jnp.bfloat16
@@ -653,24 +710,23 @@
     bias_wide = up(h[1], LANES) + up(h[2], LANES) + up(nf, LANES)
     w_shapes = [(wide, 32), (h[1], h[0] + 16), (h[2], h[1] + 16), (nf, h[2] + 16)]
 
-    flowed, sent, counts, rest, w1, w2, w3, w4 = pl.pallas_call(
+    flowed, sent, counts, where, rest, w1, w2, w3, w4 = pl.pallas_call(
         functools.partial(flow_kernel, nf, cx, cy),
-        out_shape=(jax.ShapeDtypeStruct(fields.shape, f32),
+        out_shape=(jax.ShapeDtypeStruct((nf, cells, cz), f32),
                    jax.ShapeDtypeStruct(traffic, bf16),
                    jax.ShapeDtypeStruct((size, 1, LANES), jnp.int32),
+                   jax.ShapeDtypeStruct((up(cells + 1, SUB * LANES) // LANES, LANES), jnp.int32),
                    jax.ShapeDtypeStruct((nf, LANES), f32))
         + tuple(jax.ShapeDtypeStruct(w, bf16) for w in w_shapes),
         in_specs=spec(pltpu.HBM, 11),
-        out_specs=tuple(spec(pl.ANY, 8)),
+        out_specs=tuple(spec(pl.ANY) + spec(pltpu.VMEM, 8)),
         scratch_shapes=[pltpu.SMEM((1, listed), jnp.int32)]
-        + [pltpu.VMEM((nf,) + padded, f32)] * 3 + [
-            pltpu.VMEM((3,) + padded, f32),
-            pltpu.VMEM((nf, cx, cy, cz), f32),
+        + [pltpu.VMEM((nf,) + box, f32)] * 3 + [
+            pltpu.VMEM((3,) + box, f32),
+            pltpu.VMEM((nf, room, cz), f32),
             pltpu.VMEM((6, cx, cy // SUB, SUB, cz), f32),
             pltpu.VMEM(traffic, bf16),
-            pltpu.VMEM(traffic, bf16),
             pltpu.VMEM((1, LANES), jnp.int32),
-            pltpu.VMEM((size, 1, LANES), jnp.int32),
             pltpu.VMEM((nf, h[0]), bf16),
             pltpu.VMEM((h[1], h[0]), bf16),
             pltpu.VMEM((h[2], h[1]), bf16),
@@ -682,19 +738,18 @@
             pltpu.VMEM((32, wide), f32),
             pltpu.VMEM((32, bias_wide), f32),
             pltpu.VMEM((bias_wide, 32), bf16),
-        ] + [pltpu.VMEM(w, bf16) for w in w_shapes] + [
             pltpu.VMEM((h[0] + 16, LANES), bf16),
             pltpu.VMEM((h[1] + 16, LANES), bf16),
             pltpu.VMEM((h[2] + 16, LANES), bf16),
-            pltpu.VMEM((nf, LANES), f32),
             pltpu.VMEM((2, cy, cz), f32),
             pltpu.VMEM((2, cx, cz), f32),
             pltpu.VMEM((2, cx, SUB, cz), f32),
             pltpu.VMEM((2, cx, cz), f32),
             pltpu.VMEM((cx, SUB, cz), f32),
         ] + halo_scratch(slots, cx, cy) + [
-            dma((6,)), dma((6,)), dma((chunks + 1,)), dma((chunks,)),
-            dma((chunks + 1, size)), dma((chunks + 1, size)), dma((9,)), dma((5,)), dma((2,))],
+            dma((6,)), dma((6,)), dma((chunks, 4)), dma((chunks,)),
+            dma((chunks + 1, size)), dma((chunks + 1, size)), dma((9,)),
+            pltpu.SMEM((size, 1, LANES), jnp.int32), dma],
         compiler_params=pltpu.CompilerParams(
             collective_id=0, has_side_effects=True, vmem_limit_bytes=48 * MIB),
         name="flow",
@@ -705,12 +760,11 @@
     group = 4
     n_lanes = group * LANES
     halves = size * cap // 2
-    ret, where = pl.pallas_call(
-        functools.partial(chem_kernel, nf, cells, group, size),
-        out_shape=(jax.ShapeDtypeStruct((chunks, halves, 2 * SUB, LANES), bf16),
-                   jax.ShapeDtypeStruct((cells + SUB,), jnp.int32)),
-        in_specs=spec(pltpu.SMEM, 2) + spec(pltpu.VMEM, 6),
-        out_specs=(spec(pltpu.VMEM)[0], spec(pltpu.SMEM)[0]),
+    ret = pl.pallas_call(
+        functools.partial(chem_kernel, nf, group, size),
+        out_shape=jax.ShapeDtypeStruct((chunks, halves, 2 * SUB, LANES), bf16),
+        in_specs=spec(pltpu.SMEM) + spec(pltpu.VMEM, 6),
+        out_specs=spec(pltpu.VMEM)[0],
         scratch_shapes=[
             pltpu.SMEM((size * cap + group,), jnp.int32),
             pltpu.VMEM((nf + SUB, n_lanes), f32),
@@ -722,7 +776,7 @@
         ],
         compiler_params=pltpu.CompilerParams(vmem_limit_bytes=40 * MIB),
         name="chem",
-    )(react_list[0], counts, sent.reshape(chunks, halves, 2 * SUB, LANES), rest,
+    )(counts, sent.reshape(chunks, halves, 2 * SUB, LANES), rest,
       w1, w2, w3, w4)
 
     most = max(lax.axis_size(a) for a in AXES) - 1
@@ -733,7 +787,8 @@
         in_specs=spec(pltpu.SMEM, 3) + spec(pl.ANY, 2) + spec(pltpu.VMEM),
         out_specs=(spec(pl.ANY)[0], spec(pltpu.SMEM)[0]),
         scratch_shapes=[
-            pltpu.VMEM((nf,) + padded, f32),
+            pltpu.VMEM((nf,) + box, f32),
+            pltpu.VMEM((nf, room, cz), f32),
             pltpu.VMEM((nf, cx, cy, cz), f32),
             pltpu.VMEM(traffic, bf16),
             pltpu.VMEM(traffic, bf16),

time: 111 us -> 109 us (0.982)
  Pallas kernels: 106 us -> 103 us
    pallas_call x1, Pallas kernels: 29.4 us -> 27.5 us  [local(): pl.pallas_call(functools.partial(chem_kernel, nf, group, size), out_shape...]
where the time goes in v3:
time: 109 us; the launch traced here: 107 us
  Pallas kernels  103 us (94%)
  between operations  2.37 us (2%)
  local copies, waits for them, and re-layouts  1.68 us (2%)
    pallas_call x1, Pallas kernels, local(): pl.pallas_call(functools.partial(flow_kernel, nf, cx, cy), out_shape=(jax...  51.3 us
    pallas_call x1, Pallas kernels, local(): pl.pallas_call(functools.partial(chem_kernel, nf, group, size), out_shape...  27.5 us
    pallas_call x1, Pallas kernels, local(): pl.pallas_call(functools.partial(diffuse_kernel, nf, cx, cy), out_shape=(...  24.4 us

profile of v3, /device:TPU:0, one launch (start us, length us, event | category | flops | bytes accessed | tf_op | source)
XLA Modules:
  0.0 107.3 jit_solution(15234540846479502606)
XLA Ops:
  0.6 51.3 %flow.1 = (f32[24,256,128]{2,1,0:T(8,128)}, bf16[3,16,3,16,128]{4,3,2,1,0:T(8,128)(2,1)S(1)}, s32[16,1,128]{2,1,0:T(1,128)S(1)}, s32[8,128]{1,0:T(8,128)S(1)}, f...) custom-call(s32[1,96]{1,0:T(1,128)} %list_hbm.1, ...), custom_call_target="tpu_custom_call" | custom-call | tf_op jit(solution)/shard_map/flow/pallas_call | solution.py:713
  52.0 0.0 copy-start
  52.0 0.0 copy-start.1
  52.0 27.5 %chem.1 = bf16[3,48,16,128]{3,2,1,0:T(8,128)(2,1)S(1)} custom-call(s32[16,1,128]{2,1,0:T(1,128)S(1)} %get-tuple-element.13.count_ref, bf16[3,48,16,128]{3,2,1,0:T(8,128)(2,1)S(1)} %bitcast.7, f32[24,128]{1,0:T(8,128)S(1)} %get-tuple-element.15.rest.rest_ref, bf16[1664,32]{1,0:T(8,128)(2,1)S(1)} %get-tuple-element.16.w1, ...), custom_call_target="tpu_custom_call" | custom-call | tf_op jit(solution)/shard_map/chem/pallas_call | solution.py:763
  79.5 0.0 copy-done
  79.5 0.0 copy-done.1
  79.5 24.4 %diffuse.1 = (f32[24,8,32,128]{3,2,1,0:T(8,128)S(1)}, f32[1]{0:T(128)}) custom-call(f32[24]{0:T(128)S(1)} %copy-done, s32[8,128]{1,0:T(8,128)S(1)} %get-tuple-element.11.where_ref, s32[96]{0:T(128)S(1)} %bitcast.8, f32[24,256,128]{2,1,0:T(8,128)} %get-tuple-element.12.q_hbm, bf16[3,16,3,16,128]{4,3,2,1,0:T(8,128)(2,1)S(1)} %bitcast.6, ...), custom_call_target="tpu_custom_call" | custom-call | tf_op jit(solution)/shard_map/diffuse/pallas_call | solution.py:783
  103.9 1.7 %copy.17 = f32[24,8,32,128]{3,2,1,0:T(8,128)} copy(f32[24,8,32,128]{3,2,1,0:T(8,128)S(1)} %get-tuple-element.22) | data formatting | bytes 6291456
Async XLA Ops:
  52.0 27.5 %copy-start = (f32[24]{0:T(128)S(1)}, f32[24]{0:T(128)}, u32[]{:S(2)}) copy-start(f32[24]{0:T(128)} %d_ref.1) | copy-start | bytes 292
  52.0 27.5 %copy-start.1 = (s32[1,96]{1,0:T(1,128)S(1)}, s32[1,96]{1,0:T(1,128)}, u32[]{:S(2)}) copy-start(s32[1,96]{1,0:T(1,128)} %param.25) | copy-start | bytes 1156

commit v4 on v3

--- a/solution.py
+++ b/solution.py
@@ -363,35 +363,38 @@
 
     room = flow_ref.shape[1]
     cap = 2 * sd.shape[2]
-    for copy in counts:
-        copy.wait_recv()
-    tally = pltpu.make_async_copy(cr, tally_ref, tally_sem)
-    tally.start()
-    tally.wait()
-    me = team.place()
-    ahead = lax.fori_loop(1, team.size, lambda k, n: n + jnp.where(
-        k <= me, tally_ref[k, 0, 0], 0), 0)
-    shift = lax.rem(ahead + team.size - me, team.size)
-    home = lax.broadcasted_iota(jnp.int32, where_ref.shape, 0) * LANES + (
-        lax.broadcasted_iota(jnp.int32, where_ref.shape, 1))
-    table = jnp.where(home == cells, shift, team.size * cap)
-    for e in range(listed):
-        slot = lax.rem(shift + e, team.size) * cap + e // team.size
-        table = jnp.where(home == list_ref[0, e], slot, table)
-    where_ref[...] = table
     flow2 = flow_ref.reshape(nf * room, LANES)
     sends, stores = [], []
 
-    def block(c, s, k):
+    def deal():
+        for copy in counts:
+            copy.wait_recv()
+        tally = pltpu.make_async_copy(cr, tally_ref, tally_sem)
+        tally.start()
+        tally.wait()
+        me = team.place()
+        ahead = lax.fori_loop(1, team.size, lambda k, n: n + jnp.where(
+            k <= me, tally_ref[k, 0, 0], 0), 0)
+        shift = lax.rem(ahead + team.size - me, team.size)
+        home = lax.broadcasted_iota(jnp.int32, where_ref.shape, 0) * LANES + (
+            lax.broadcasted_iota(jnp.int32, where_ref.shape, 1))
+        table = jnp.where(home == cells, shift, team.size * cap)
+        for e in range(listed):
+            slot = lax.rem(shift + e, team.size) * cap + e // team.size
+            table = jnp.where(home == list_ref[0, e], slot, table)
+        where_ref[...] = table
+        return shift
+
+    def block(c, s, k, shift):
         e = s * team.size + lax.rem(k + team.size - shift, team.size)
         b = jnp.maximum(list_ref[0, jnp.minimum(e, listed - 1)], 0)
         return flow2[pl.ds(c * SUB * room + b, SUB, stride=room), :]
 
-    def dispatch(c):
+    def dispatch(c, shift):
         for k in range(team.size):
             dst = sd if k else rv
             for p in range(sd.shape[2]):
-                pair = [block(c, 2 * p + h, k) for h in range(2)]
+                pair = [block(c, 2 * p + h, k, shift) for h in range(2)]
                 dst[c, k, p] = jnp.concatenate(pair, axis=0).astype(jnp.bfloat16)
         for k in range(1, team.size):
             sends.append(remote(sd.at[c, k], rv.at[c, k], team_send.at[c, k],
@@ -401,6 +404,8 @@
     for stage in range(3):
         weight = (1.0 / 3.0, 0.5, 1.0)[stage]
         u = us[stage]
+        if stage == 1:
+            shift = deal()
         for c in range(chunks):
             slot = stage * chunks + c
             first = c * SUB
@@ -440,7 +445,7 @@
                 halo.send_x(slot + chunks)
                 halo.send_yz(slot + chunks, us[stage + 1], first)
             else:
-                dispatch(c)
+                dispatch(c, shift)
                 part = pl.ds(first, SUB)
                 stores.append(pltpu.make_async_copy(
                     flow_ref.at[part, pl.ds(0, cells)], out_hbm.at[part], out_sem.at[c]))
@@ -499,41 +504,46 @@
 
     count = lax.fori_loop(0, size, pick, (0, 0))[1]
 
-    def run(g, _):
-        base = g * group
-        for i in range(group):
+    def run(base, blocks):
+        part = pl.ds(0, blocks * LANES)
+        for i in range(blocks):
             slot = jnp.where(base + i < count, todo[base + i], 0)
             for c in range(chunks):
                 tile = slots[c, slot // 2].astype(jnp.float32)
                 x_in[c * SUB:(c + 1) * SUB, i * LANES:(i + 1) * LANES] = jnp.where(
                     lax.rem(slot, 2) == 0, tile[:SUB], tile[SUB:])
-        inc[...] = network(x_in[...].astype(jnp.bfloat16), w1, w2, w3, w4, h1, h2, h3)
-        for i in range(group):
+        inc[:, part] = network(x_in[:, part].astype(jnp.bfloat16), w1, w2, w3, w4,
+                               h1.at[:, part], h2.at[:, part], h3.at[:, part])
+        for i in range(blocks):
             slot = jnp.where(base + i < count, todo[base + i], size * cap)
             for c in range(chunks):
                 res[c, slot] = inc[c * SUB:(c + 1) * SUB, i * LANES:(i + 1) * LANES] - rest[
                     c * SUB:(c + 1) * SUB]
-        return 0
-
-    lax.fori_loop(0, (count + group - 1) // group, run, 0)
+
+    tail = group // 2
+    full = (count + tail - 1) // group
+    lax.fori_loop(0, full, lambda g, n: (run(g * group, group), n)[1], 0)
+
+    @pl.when(full * group < count)
+    def _():
+        run(full * group, tail)
+
     for c in range(chunks):
         for p in range(halves):
             pair = jnp.concatenate([res[c, 2 * p], res[c, 2 * p + 1]], axis=0)
             ret_ref[c, p] = pair.astype(jnp.bfloat16)
 
 
-def diffuse_kernel(nf, cx, cy, d_ref, where_ref, owner_ref, q_hbm, ret_hbm, rest_ref, out_hbm, act_out,
-                   u_ref, old_ref, new_ref, ret, got_ret, res, part, got, act_send, act_recv,
+def diffuse_kernel(nf, cx, cy, d_ref, where_ref, owner_ref, q_hbm, ret, rest_ref, out_hbm, act_out,
+                   u_ref, old_ref, new_ref, got_ret, res, part, got, act_send, act_recv,
                    xs, xr, ys, yr, zs, zr, send_sem, recv_sem,
-                   team_send, team_recv, in_sem, out_sem, ret_sem):
+                   team_send, team_recv, in_sem, out_sem):
     grid = Grid(cx, cy)
     chunks = nf // SUB
     team = Team()
     pairs = ret.shape[2]
     cells = cx * cy
     cap = 2 * pairs
-    own = pltpu.make_async_copy(ret_hbm, ret, ret_sem)
-    own.start()
     loads = []
     for c in range(chunks):
         loads.append(pltpu.make_async_copy(
@@ -550,7 +560,6 @@
     u2 = u_ref.reshape(nf * grid.px * grid.py, LANES)
     room = old_ref.shape[1]
     old2 = old_ref.reshape(nf * room, LANES)
-    own.wait()
     met(known)
     backs = [[remote(ret.at[c, k], got_ret.at[c, k], team_send.at[c, k], team_recv.at[c, k],
                      members[k]) for k in range(1, team.size)] for c in range(chunks)]
@@ -621,10 +630,9 @@
         halo.send_x(c)
         halo.load_z(c, u2, c * SUB)
         halo.send_yz(c, u2, c * SUB)
-        if c == 0:
-            part[0] = heat()
-            for h in hops(0):
-                h.start()
+    part[0] = heat()
+    for h in hops(0):
+        h.start()
     stores = []
     for c in range(chunks):
         if c < len(groups) - 1:
@@ -757,7 +765,7 @@
         react_list, fields, velocity, weight_in, weight_mid.T, weight_low.T, weight_out.T,
         bias_in, bias_mid, bias_low, bias_out)])
 
-    group = 4
+    group = 8
     n_lanes = group * LANES
     halves = size * cap // 2
     ret = pl.pallas_call(
@@ -766,7 +774,7 @@
         in_specs=spec(pltpu.SMEM) + spec(pltpu.VMEM, 6),
         out_specs=spec(pltpu.VMEM)[0],
         scratch_shapes=[
-            pltpu.SMEM((size * cap + group,), jnp.int32),
+            pltpu.SMEM((size * cap + 2 * group,), jnp.int32),
             pltpu.VMEM((nf + SUB, n_lanes), f32),
             pltpu.VMEM((h[0] + 16, n_lanes), bf16),
             pltpu.VMEM((h[1] + 16, n_lanes), bf16),
@@ -784,13 +792,12 @@
         functools.partial(diffuse_kernel, nf, cx, cy),
         out_shape=(jax.ShapeDtypeStruct(fields.shape, f32),
                    jax.ShapeDtypeStruct((1,), f32)),
-        in_specs=spec(pltpu.SMEM, 3) + spec(pl.ANY, 2) + spec(pltpu.VMEM),
+        in_specs=spec(pltpu.SMEM, 3) + spec(pl.ANY) + spec(pltpu.VMEM, 2),
         out_specs=(spec(pl.ANY)[0], spec(pltpu.SMEM)[0]),
         scratch_shapes=[
             pltpu.VMEM((nf,) + box, f32),
             pltpu.VMEM((nf, room, cz), f32),
             pltpu.VMEM((nf, cx, cy, cz), f32),
-            pltpu.VMEM(traffic, bf16),
             pltpu.VMEM(traffic, bf16),
             pltpu.VMEM((chunks, size * cap + 1, SUB, LANES), f32),
             pltpu.VMEM((len(AXES), SUB, LANES), f32),
@@ -798,7 +805,7 @@
             dma((len(AXES), most)),
             dma((len(AXES), most)),
         ] + halo_scratch(chunks, cx, cy) + [
-            dma((chunks, size)), dma((chunks, size)), dma((chunks,)), dma((chunks,)), dma],
+            dma((chunks, size)), dma((chunks, size)), dma((chunks,)), dma((chunks,))],
         compiler_params=pltpu.CompilerParams(
             collective_id=1, has_side_effects=True, vmem_limit_bytes=48 * MIB),
         name="diffuse",

time: 109 us -> 108 us (level); the launches traced: 107 us -> 109 us
  Pallas kernels: 103 us -> 105 us
    pallas_call x1, Pallas kernels: 27.5 us -> 29.4 us  [local(): pl.pallas_call(functools.partial(chem_kernel, nf, group, size), out_shape...]
    pallas_call x1, Pallas kernels: 51.3 us -> 50.2 us  [local(): pl.pallas_call(functools.partial(flow_kernel, nf, cx, cy), out_shape=(jax...]
where the time goes in v4:
time: 108 us; the launch traced here: 109 us
  Pallas kernels  105 us (97%)
  between operations  2.37 us (2%)
  local copies, waits for them, and re-layouts  1.68 us (2%)
    pallas_call x1, Pallas kernels, local(): pl.pallas_call(functools.partial(flow_kernel, nf, cx, cy), out_shape=(jax...  50.2 us
    pallas_call x1, Pallas kernels, local(): pl.pallas_call(functools.partial(chem_kernel, nf, group, size), out_shape...  29.4 us
    pallas_call x1, Pallas kernels, local(): pl.pallas_call(functools.partial(diffuse_kernel, nf, cx, cy), out_shape=(...  25 us

profile of v4, /device:TPU:0, one launch (start us, length us, event | category | flops | bytes accessed | tf_op | source)
XLA Modules:
  0.0 108.6 jit_solution(8148782040592004644)
XLA Ops:
  0.6 50.2 %flow.1 = (f32[24,256,128]{2,1,0:T(8,128)}, bf16[3,16,3,16,128]{4,3,2,1,0:T(8,128)(2,1)S(1)}, s32[16,1,128]{2,1,0:T(1,128)S(1)}, s32[8,128]{1,0:T(8,128)S(1)}, f...) custom-call(s32[1,96]{1,0:T(1,128)} %list_hbm.1, ...), custom_call_target="tpu_custom_call" | custom-call | tf_op jit(solution)/shard_map/flow/pallas_call | solution.py:721
  50.9 0.0 copy-start
  50.9 0.0 copy-start.1
  50.9 29.4 %chem.1 = bf16[3,48,16,128]{3,2,1,0:T(8,128)(2,1)S(1)} custom-call(s32[16,1,128]{2,1,0:T(1,128)S(1)} %get-tuple-element.13.count_ref, bf16[3,48,16,128]{3,2,1,0:T(8,128)(2,1)S(1)} %bitcast.7, f32[24,128]{1,0:T(8,128)S(1)} %get-tuple-element.15.rest.rest_ref, bf16[1664,32]{1,0:T(8,128)(2,1)S(1)} %get-tuple-element.16.w1, ...), custom_call_target="tpu_custom_call" | custom-call | tf_op jit(solution)/shard_map/chem/pallas_call | solution.py:771
  80.3 0.0 copy-done
  80.3 0.0 copy-done.1
  80.3 25.0 %diffuse.1 = (f32[24,8,32,128]{3,2,1,0:T(8,128)S(1)}, f32[1]{0:T(128)}) custom-call(f32[24]{0:T(128)S(1)} %copy-done, s32[8,128]{1,0:T(8,128)S(1)} %get-tuple-element.11.where_ref, s32[96]{0:T(128)S(1)} %bitcast.8, f32[24,256,128]{2,1,0:T(8,128)} %get-tuple-element.12.q_hbm, bf16[3,16,3,16,128]{4,3,2,1,0:T(8,128)(2,1)S(1)} %bitcast.6, ...), custom_call_target="tpu_custom_call" | custom-call | tf_op jit(solution)/shard_map/diffuse/pallas_call | solution.py:791
  105.3 1.7 %copy.17 = f32[24,8,32,128]{3,2,1,0:T(8,128)} copy(f32[24,8,32,128]{3,2,1,0:T(8,128)S(1)} %get-tuple-element.22) | data formatting | bytes 6291456
Async XLA Ops:
  50.9 29.4 %copy-start = (f32[24]{0:T(128)S(1)}, f32[24]{0:T(128)}, u32[]{:S(2)}) copy-start(f32[24]{0:T(128)} %d_ref.1) | copy-start | bytes 292
  50.9 29.4 %copy-start.1 = (s32[1,96]{1,0:T(1,128)S(1)}, s32[1,96]{1,0:T(1,128)}, u32[]{:S(2)}) copy-start(s32[1,96]{1,0:T(1,128)} %param.25) | copy-start | bytes 1156

commit v5 on v4

--- a/solution.py
+++ b/solution.py
@@ -250,7 +250,7 @@
     w_loads = [pltpu.make_async_copy(src, dst, w_in.at[i]) for i, (src, dst) in enumerate((
         (wi_hbm, wi), (b1_hbm, b1), (b2_hbm, b2), (b3_hbm, b3), (b4_hbm, b4),
         (wo_hbm, wo), (list_hbm, list_ref), (wl_hbm, wl), (wm_hbm, wm)))]
-    for copy in sum(faces, []) + [v_load] + inner:
+    for copy in sum(faces, []) + [v_load] + inner + w_loads:
         copy.start()
     near = neighbours()
     (xu, xd), (yu, yd), (zu, zd) = near
@@ -295,8 +295,6 @@
         copy.start()
     for copy in inner:
         copy.wait()
-    for copy in w_loads:
-        copy.start()
     for c in range(chunks):
         halo.load_z(c, us[0], c * SUB)
         halo.send_yz(c, us[0], c * SUB)
@@ -325,11 +323,6 @@
     widen(w2, wm, 0.5, cols, 0)
     widen(w3, wl, 0.5, cols, n2)
     widen(w4, wo, 1.0, cols, n2 + n3)
-    for h in (h1, h2, h3):
-        h[h.shape[0] - 16:] = bias_ones(16, LANES).astype(jnp.bfloat16)
-    origin = jnp.concatenate(
-        [jnp.zeros((nf, LANES), jnp.float32), bias_ones(w1.shape[1] - nf, LANES)], axis=0)
-    rest[...] = network(origin.astype(jnp.bfloat16), w1, w2, w3, w4, h1, h2, h3)
 
     for copy in v_copies:
         copy.wait_recv()
@@ -366,6 +359,13 @@
     flow2 = flow_ref.reshape(nf * room, LANES)
     sends, stores = [], []
 
+    def settle():
+        for h in (h1, h2, h3):
+            h[h.shape[0] - 16:] = bias_ones(16, LANES).astype(jnp.bfloat16)
+        origin = jnp.concatenate(
+            [jnp.zeros((nf, LANES), jnp.float32), bias_ones(w1.shape[1] - nf, LANES)], axis=0)
+        rest[...] = network(origin.astype(jnp.bfloat16), w1, w2, w3, w4, h1, h2, h3)
+
     def deal():
         for copy in counts:
             copy.wait_recv()
@@ -406,6 +406,8 @@
         u = us[stage]
         if stage == 1:
             shift = deal()
+        if stage == 2:
+            settle()
         for c in range(chunks):
             slot = stage * chunks + c
             first = c * SUB

time: 108 us -> 105 us (0.972)
  Pallas kernels: 105 us -> 101 us
    pallas_call x1, Pallas kernels: 29.4 us -> 19.2 us  [local(): pl.pallas_call(functools.partial(chem_kernel, nf, group, size), out_shape...]
    pallas_call x1, Pallas kernels: 25 us -> 32.6 us  [local(): pl.pallas_call(functools.partial(diffuse_kernel, nf, cx, cy), out_shape=(...]
    pallas_call x1, Pallas kernels: 50.2 us -> 48.9 us  [local(): pl.pallas_call(functools.partial(flow_kernel, nf, cx, cy), out_shape=(jax...]
where the time goes in v5:
time: 105 us
  Pallas kernels  101 us (96%)
  between operations  2.37 us (2%)
  local copies, waits for them, and re-layouts  1.68 us (2%)
    pallas_call x1, Pallas kernels, local(): pl.pallas_call(functools.partial(flow_kernel, nf, cx, cy), out_shape=(jax...  48.9 us
    pallas_call x1, Pallas kernels, local(): pl.pallas_call(functools.partial(diffuse_kernel, nf, cx, cy), out_shape=(...  32.6 us
    pallas_call x1, Pallas kernels, local(): pl.pallas_call(functools.partial(chem_kernel, nf, group, size), out_shape...  19.2 us

profile of v5, /device:TPU:0, one launch (start us, length us, event | category | flops | bytes accessed | tf_op | source)
XLA Modules:
  0.0 104.8 jit_solution(14935625602859454361)
XLA Ops:
  0.6 48.9 %flow.1 = (f32[24,256,128]{2,1,0:T(8,128)}, bf16[3,16,3,16,128]{4,3,2,1,0:T(8,128)(2,1)S(1)}, s32[16,1,128]{2,1,0:T(1,128)S(1)}, s32[8,128]{1,0:T(8,128)S(1)}, f...) custom-call(s32[1,96]{1,0:T(1,128)} %list_hbm.1, ...), custom_call_target="tpu_custom_call" | custom-call | tf_op jit(solution)/shard_map/flow/pallas_call | solution.py:723
  49.5 0.0 copy-start
  49.5 0.0 copy-start.1
  49.5 19.2 %chem.1 = bf16[3,48,16,128]{3,2,1,0:T(8,128)(2,1)S(1)} custom-call(s32[16,1,128]{2,1,0:T(1,128)S(1)} %get-tuple-element.13.count_ref, bf16[3,48,16,128]{3,2,1,0:T(8,128)(2,1)S(1)} %bitcast.7, f32[24,128]{1,0:T(8,128)S(1)} %get-tuple-element.15.rest.rest_ref, bf16[1664,32]{1,0:T(8,128)(2,1)S(1)} %get-tuple-element.16.w1, ...), custom_call_target="tpu_custom_call" | custom-call | tf_op jit(solution)/shard_map/chem/pallas_call | solution.py:773
  68.7 0.0 copy-done
  68.8 0.0 copy-done.1
  68.8 32.6 %diffuse.1 = (f32[24,8,32,128]{3,2,1,0:T(8,128)S(1)}, f32[1]{0:T(128)}) custom-call(f32[24]{0:T(128)S(1)} %copy-done, s32[8,128]{1,0:T(8,128)S(1)} %get-tuple-element.11.where_ref, s32[96]{0:T(128)S(1)} %bitcast.8, f32[24,256,128]{2,1,0:T(8,128)} %get-tuple-element.12.q_hbm, bf16[3,16,3,16,128]{4,3,2,1,0:T(8,128)(2,1)S(1)} %bitcast.6, ...), custom_call_target="tpu_custom_call" | custom-call | tf_op jit(solution)/shard_map/diffuse/pallas_call | solution.py:793
  101.4 1.7 %copy.17 = f32[24,8,32,128]{3,2,1,0:T(8,128)} copy(f32[24,8,32,128]{3,2,1,0:T(8,128)S(1)} %get-tuple-element.22) | data formatting | bytes 6291456
Async XLA Ops:
  49.5 19.2 %copy-start = (f32[24]{0:T(128)S(1)}, f32[24]{0:T(128)}, u32[]{:S(2)}) copy-start(f32[24]{0:T(128)} %d_ref.1) | copy-start | bytes 292
  49.5 19.2 %copy-start.1 = (s32[1,96]{1,0:T(1,128)S(1)}, s32[1,96]{1,0:T(1,128)}, u32[]{:S(2)}) copy-start(s32[1,96]{1,0:T(1,128)} %param.25) | copy-start | bytes 1156
